TPU v7x, 32 devices: a whole 2x2x4 slice. The times are simulated.
32 devices in a mesh: row: 8 (over z, y), col: 4 (over x, core).
Axes of the slice: x: 2, y: 2, z: 4, core: 2. Of those that a mesh axis runs over, the one named last changes fastest.
Arguments:
- load_currents: float32 [32, 1024, 512], P(None, 'row', 'col'), may hold values from -36 to 36
- labels: int32 [1024, 512], P('row', 'col'), may hold values from 0 to 255, as said below
- bump_height: float32 [1024, 512], P('row', 'col'), may hold values from 0.5 to 2
- horizontal_class: int32 [1024, 512], P('row', 'col'), may hold values from 0 to 7
- vertical_class: int32 [1024, 512], P('row', 'col'), may hold values from 0 to 7
- pad_class: int32 [1024, 512], P('row', 'col'), may hold values from 0 to 7
- edge_table: float32 [8], replicated, may hold values from 0.5 to 4
- pad_table: float32 [8], replicated, may hold values from 0.02 to 0.5
Outputs:
- solution: float32 [32, 1024, 512], P(None, 'row', 'col')
- residual: float32 [32, 1024, 512], P(None, 'row', 'col')
Inputs may be any that keep to these rules, and one draw needn't show every extreme that they name: `labels`: every number from 0 to 255 is the label of some nodes; the label of node (i, j) is 16 * floor(16 * i2 / 1024) + floor(16 * j2 / 512) for some node (i2, j2) of the grid with |i2 - i| <= 16 and |j2 - j| <= 8.
All inputs are finite; a program needn't handle non-finite values.
Results may differ from a plain program's by a relative error of at most 0.0003.
Values sent between devices are 32-bit elements; how exact they have to be, the bound alone decides.
A program may use at most 128 MiB of HBM per device.

v0:
```python
import jax
import jax.numpy as jnp
from jax import lax
from jax.sharding import PartitionSpec as P

REG = 16
ITERS = 2


precise = lax.Precision.HIGHEST


def from_behind(value, axis, steps):
    count = lax.axis_size(axis)
    initial, last = (max(0, -steps), min(count, count - steps))
    return lax.ppermute(value, axis, [(source, source + steps) for source in range(initial, last)])


def extended(value, sides, width):
    for axis, dim in sides:
        size, length = (lax.axis_size(axis), value.shape[dim])
        up = [(i, (i + 1) % size) for i in range(size - 1)]
        down = [(j, i) for i, j in up]
        last = lax.slice_in_dim(value, length - width, length, axis=dim)
        initial = lax.slice_in_dim(value, 0, width, axis=dim)
        before = lax.ppermute(last, axis, up)
        after = lax.ppermute(initial, axis, down)
        value = jnp.concatenate([before, value, after], axis=dim)
    return value


def lookup(entries, classes):
    levels = lax.broadcasted_iota(jnp.int32, (entries.shape[0],) + classes.shape, 0)
    return jnp.sum(jnp.where(classes[None] == levels, entries[:, None, None], 0.0), axis=0)


def stencil(padded, coeffs):
    diagonal, right_link, left_link, down_link, upper_link = coeffs
    centre = padded[:, 1:-1, 1:-1]
    return (
        diagonal * centre
        - right_link * padded[:, 1:-1, 2:]
        - left_link * padded[:, 1:-1, :-2]
        - down_link * padded[:, 2:, 1:-1]
        - upper_link * padded[:, :-2, 1:-1]
    )


def invert(matrix):
    factor = jnp.linalg.cholesky(matrix)
    identity = jnp.eye(matrix.shape[0], dtype=matrix.dtype)
    lower_solved = lax.linalg.triangular_solve(factor, identity, left_side=True, lower=True)
    return lax.linalg.triangular_solve(
        factor, lower_solved, left_side=True, lower=True, transpose_a=True
    )


def body(
    load_currents,
    labels,
    bump_height,
    horizontal_class,
    vertical_class,
    pad_class,
    edge_table,
    pad_table,
):
    tile_rows, tile_cols = labels.shape
    regions = REG * REG
    load_count = load_currents.shape[0]
    tile_cells = tile_rows * tile_cols
    grid_rows = lax.axis_size("row") * tile_rows
    grid_cols = lax.axis_size("col") * tile_cols
    row_ids = lax.axis_index("row") * tile_rows + lax.broadcasted_iota(jnp.int32, labels.shape, 0)
    col_ids = lax.axis_index("col") * tile_cols + lax.broadcasted_iota(jnp.int32, labels.shape, 1)
    right_link = jnp.where(col_ids == grid_cols - 1, 0.0, lookup(edge_table, horizontal_class))
    down_link = jnp.where(row_ids == grid_rows - 1, 0.0, lookup(edge_table, vertical_class))
    left_edge = from_behind(right_link[:, -1:], "col", 1)
    left_link = jnp.concatenate([left_edge, right_link[:, :-1]], axis=1)
    upper_edge = from_behind(down_link[-1:, :], "row", 1)
    upper_link = jnp.concatenate([upper_edge, down_link[:-1, :]], axis=0)
    diagonal = lookup(pad_table, pad_class) + right_link + left_link + down_link + upper_link
    coeffs = (diagonal, right_link, left_link, down_link, upper_link)
    levels = lax.broadcasted_iota(jnp.int32, (regions,) + labels.shape, 0)
    deflation = jnp.where(labels[None] == levels, bump_height[None], 0.0)
    deflation_image = stencil(extended(deflation, (("row", 1), ("col", 2)), 1), coeffs)
    basis_flat = deflation.reshape(regions, tile_cells)
    image_flat = deflation_image.reshape(regions, tile_cells)
    contract = (((1,), (1,)), ((), ()))
    partial_matrix = lax.dot_general(basis_flat, image_flat, contract, precision=precise)
    inverse = invert(lax.psum(partial_matrix, ("row", "col")))

    def project(field):
        return lax.dot_general(
            field.reshape(load_count, tile_cells), basis_flat, contract, precision=precise
        )

    def expand(coarse):
        return jnp.dot(coarse, basis_flat, precision=precise).reshape(
            load_count, tile_rows, tile_cols
        )

    def correction_image(coarse):
        return jnp.dot(coarse, image_flat, precision=precise).reshape(
            load_count, tile_rows, tile_cols
        )

    def refresh(residual):
        scaled = residual / diagonal
        local_norm = jnp.sum(residual * scaled, axis=(1, 2))
        field_image = stencil(extended(scaled, (("row", 1), ("col", 2)), 1), coeffs)
        weighted_norm = lax.psum(local_norm, ("row", "col"))
        projected = lax.psum(project(field_image), ("row", "col"))
        coarse = jnp.dot(projected, inverse, precision=precise)
        return (scaled, weighted_norm, field_image, coarse)

    load_sums = lax.psum(project(load_currents), ("row", "col"))
    coarse = jnp.dot(load_sums, inverse, precision=precise)
    solution = expand(coarse)
    residual = load_currents - correction_image(coarse)
    scaled, weighted_norm, field_image, coarse = refresh(residual)
    spread = expand(coarse)
    direction = scaled - spread
    direction_image = field_image - correction_image(coarse)
    for iteration in range(ITERS):
        local_curve = jnp.sum(direction * direction_image, axis=(1, 2))
        curvature = lax.psum(local_curve, ("row", "col"))
        step_size = (weighted_norm / curvature)[:, None, None]
        solution = solution + step_size * direction
        residual = residual - step_size * direction_image
        if iteration + 1 < ITERS:
            scaled, new_norm, field_image, coarse = refresh(residual)
            spread = expand(coarse)
            beta_ratio = (new_norm / weighted_norm)[:, None, None]
            direction = scaled - spread + beta_ratio * direction
            direction_image = field_image - correction_image(coarse) + beta_ratio * direction_image
            weighted_norm = new_norm
    return (solution, residual)


def solution(mesh):
    return jax.shard_map(
        body,
        mesh=mesh,
        in_specs=(
            P(None, "row", "col"),
            P("row", "col"),
            P("row", "col"),
            P("row", "col"),
            P("row", "col"),
            P("row", "col"),
            P(),
            P(),
        ),
        out_specs=(P(None, "row", "col"), P(None, "row", "col")),
        check_vma=False,
    )
```

profile of v0, /device:TPU:0, one launch (start us, length us, event | category | flops | bytes accessed | tf_op | source)
XLA Modules:
  0.0 716.1 jit_solution(5788398756781292680)
XLA Ops:
  11.0 4.4 collective-permute-start.1
  15.3 5.4 fusion.28
  20.8 3.4 collective-permute-start.2
  25.7 18.0 %fusion.84 = f32[32,256]{1,0:T(8,128)S(1)} fusion(f32[32,128,128]{2,1,0:T(8,128)S(1)} %copy-done.11, f32[128,128]{1,0:T(8,128)S(1)} %copy-done.12, s32[128,128]{1,0:T(8,128)S(1)} %copy-done.13), kind=kOutput, calls=%fused_computation.114 | convolution fusion | flops 1619001344 | bytes 2260992 | tf_op jit(solution)/shard_map/dot_general | solution.py:94
  45.4 3.8 collective-permute-start.5
  50.1 31.3 %fusion.17 = f32[256,128,128]{0,2,1:T(8,128)S(1)} fusion(f32[256,128,128]{0,2,1:T(8,128)} %copy-done.1, f32[256,1,128]{0,2,1:T(8,128)S(1)} %collective-permute-done.2, f32[256,1,128]{0,2,1:T(8,128)S(1)} %collective-permute-done.3, f32[256,130,1]{0,2,1:T(1,128)S(1)} %collective-permute-done.5, f32[256,130,1]{0,2,1:T(1,128)S(1)} %collective-permute-done.4, ...), kind=kLoop, calls=%fused_computation.20 | loop fusion | flops 79691776 | bytes 34541568 | tf_op jit(solution)/shard_map/sub | solution.py:41
  81.5 5.7 copy-done
  87.2 38.4 %fusion.81 = f32[256,256]{0,1:T(8,128)} fusion(f32[256,128,128]{0,2,1:T(8,128)S(1)} %fusion.17, f32[128,128]{1,0:T(8,128)S(1)} %copy-done.12, s32[128,128]{1,0:T(8,128)S(1)} %copy-done.13), kind=kOutput, calls=%fused_computation.110 | convolution fusion | flops 12893290496 | bytes 17170432 | tf_op jit(solution)/shard_map/dot_general | solution.py:90
  125.7 45.2 %psum.56 = f32[32,256]{1,0:T(8,128)S(1)} all-reduce(f32[32,256]{1,0:T(8,128)S(1)} %fusion.84), channel_id=1, replica_groups=mesh['row'=8,'col'=4] {'row','col'}, use_global_device_ids=true, to_apply=%region_0.1 | all-reduce | flops 8192 | bytes 65536 | tf_op jit(solution)/shard_map/psum | solution.py:117
  170.9 87.1 %all-reduce.5.cloned.1.call-done = f32[256,256]{0,1:T(8,128)} async-done(((f32[256,256]{0,1:T(8,128)}), f32[256,256]{0,1:T(8,128)}) %all-reduce.5.cloned.1.call-update) | async-done | bytes 262160 | tf_op jit(solution)/shard_map/psum | solution.py:91
  260.1 11.7 %cholesky.53 = f32[128,128]{1,0:T(8,128)S(1)} custom-call(f32[128,128]{1,0:T(8,128)S(1)} %cholesky.121), custom_call_target="Cholesky" | custom-call | tf_op jit(solution)/shard_map/jit(cholesky)/cholesky | solution.py:50
  271.9 9.8 %custom-call.16 = f32[1,128,128]{1,2,0:T(8,128)S(1)} custom-call(f32[1,128,128]{2,1,0:T(8,128)S(1)} %get-tuple-element.56), custom_call_target="InvertDiagBlocksLowerTriangular" | custom-call | tf_op jit(solution)/shard_map/jit(cholesky)/cholesky | solution.py:50
  282.2 11.7 %cholesky.108 = f32[128,128]{1,0:T(8,128)S(1)} custom-call(f32[128,128]{1,0:T(8,128)S(1)} %convolution_subtract_fusion.2), custom_call_target="Cholesky" | custom-call | tf_op jit(solution)/shard_map/jit(cholesky)/cholesky | solution.py:50
  296.1 4.1 while.1
  300.2 20.1 %custom-call.17 = f32[2,128,128]{1,2,0:T(8,128)S(1)} custom-call(f32[2,128,128]{2,1,0:T(8,128)S(1)} %get-tuple-element.9), custom_call_target="InvertDiagBlocksLowerTriangular" | custom-call | tf_op jit(solution)/shard_map/triangular_solve | solution.py:53
  322.2 18.5 %multiply_reduce_fusion.3 = (f32[32]{0:T(128)S(1)}, f32[32,128,128]{2,0,1:T(8,128)S(1)}, f32[32,128,128]{2,0,1:T(8,128)}) fusion(f32[128,128]{1,0:T(8,128)S(1)} %get-tuple-element.34, f32[32,256,1]{1,0,2:T(8,128)S(1)} %convolution_bitcast_fusion.2, f32[256,128,128]{0,2,1:T(8,128)} %copy-done, f32[32,128,128]{2,1,0:T(8,128)} %param.8), kind=kOutput, calls=%fused_computation.105 | convolution fusion | flops 1612709888 | bytes 23167104 | tf_op jit(solution)/shard_map/dot_general | solution.py:104
  340.7 3.4 collective-permute-start.6
  345.5 4.2 collective-permute-done.7
  349.9 2.7 fusion.119
  352.7 3.2 copy.48
  357.2 3.2 copy.50
  360.4 3.2 collective-permute-start.9
  363.6 3.6 copy.49
  367.1 3.6 copy.51
  370.7 4.6 fusion.59
  376.7 16.4 %fusion.89 = f32[32,256]{1,0:T(8,128)S(1)} fusion(f32[32,128,128]{2,0,1:T(8,128)S(1)} %fusion.59, f32[128,128]{1,0:T(8,128)S(1)} %copy-done.12, s32[128,128]{1,0:T(8,128)S(1)} %copy-done.13), kind=kOutput, calls=%fused_computation.115 | convolution fusion | flops 1619001344 | bytes 2260992 | tf_op jit(solution)/shard_map/dot_general | solution.py:94
  393.1 40.3 %psum.59 = f32[32,256]{1,0:T(8,128)S(1)} all-reduce(f32[32,256]{1,0:T(8,128)S(1)} %fusion.89), channel_id=1, replica_groups=mesh['row'=8,'col'=4] {'row','col'}, use_global_device_ids=true, to_apply=%region_11.12 | all-reduce | flops 8192 | bytes 65536 | tf_op jit(solution)/shard_map/psum | solution.py:113
  433.7 17.8 %fusion.76 = f32[32,128,128]{2,0,1:T(8,128)S(1)} fusion(f32[32,128,128]{2,0,1:T(8,128)} %copy-done.10, f32[32,256,1]{1,0,2:T(8,128)S(1)} %convolution_bitcast_fusion.1, f32[256,128,128]{0,2,1:T(8,128)} %copy-done), kind=kOutput, calls=%fused_computation.109 | convolution fusion | flops 1611137024 | bytes 21004288 | tf_op jit(solution)/shard_map/dot_general | solution.py:104
  451.6 20.1 %multiply_reduce_fusion.2 = (f32[32]{0:T(128)S(1)}, f32[32,128,128]{2,0,1:T(8,128)}) fusion(f32[32,128,128]{2,0,1:T(8,128)S(1)} %fusion.76, f32[32,256,1]{1,0,2:T(8,128)S(1)} %convolution_bitcast_fusion.1, f32[128,128]{1,0:T(8,128)S(1)} %copy-done.12, s32[128,128]{1,0:T(8,128)S(1)} %copy-done.13, f32[32,128,128]{2,0,1:T(8,128)S(1)} %copy-done.8, ...), kind=kOutput, calls=%fused_computation.104 | convolution fusion | flops 1621098496 | bytes 6520960 | tf_op jit(solution)/shard_map/dot_general | solution.py:99
  471.6 39.8 %all-reduce.2 = (f32[32]{0:T(128)S(1)}, f32[32]{0:T(128)S(1)}) all-reduce(f32[32]{0:T(128)S(1)} %get-tuple-element.43, f32[32]{0:T(128)S(1)} %get-tuple-element.60), channel_id=1, replica_groups=mesh['row'=8,'col'=4] {'row','col'}, use_global_device_ids=true, to_apply=%region_10.11 | all-reduce | flops 64 | bytes 512 | tf_op jit(solution)/shard_map/psum | solution.py:112
  511.5 2.4 multiply_reduce_fusion.1
  515.2 4.2 collective-permute-start.10
  520.9 4.1 collective-permute-done.11
  525.2 2.7 fusion.118
  527.9 3.2 copy.53
  532.5 3.2 copy.55
  535.7 3.0 collective-permute-start.13
  538.7 3.6 copy.54
  542.3 3.6 copy.56
  545.9 4.6 fusion.51
  550.5 16.5 %fusion.92 = f32[32,256]{1,0:T(8,128)S(1)} fusion(f32[32,128,128]{2,0,1:T(8,128)S(1)} %fusion.51, f32[128,128]{1,0:T(8,128)S(1)} %copy-done.12, s32[128,128]{1,0:T(8,128)S(1)} %copy-done.13), kind=kOutput, calls=%fused_computation.116 | convolution fusion | flops 1619001344 | bytes 2260992 | tf_op jit(solution)/shard_map/dot_general | solution.py:94
  567.0 40.7 %all-reduce.1 = (f32[32,256]{1,0:T(8,128)S(1)}, f32[32]{0:T(128)S(1)}) all-reduce(f32[32,256]{1,0:T(8,128)S(1)} %fusion.92, f32[32]{0:T(128)S(1)} %get-tuple-element.32), channel_id=1, replica_groups=mesh['row'=8,'col'=4] {'row','col'}, use_global_device_ids=true, to_apply=%region_16.17 | all-reduce | flops 8224 | bytes 65792 | tf_op jit(solution)/shard_map/psum | solution.py:113
  608.0 17.9 %multiply_add_fusion.1 = f32[32,128,128]{2,0,1:T(8,128)S(1)} fusion(f32[32,128,128]{2,0,1:T(8,128)S(1)} %copy-done.3, f32[32,128,128]{2,0,1:T(8,128)} %copy-done.9, f32[32,256,1]{1,0,2:T(8,128)S(1)} %convolution_bitcast_fusion, f32[256,128,128]{0,2,1:T(8,128)} %copy-done, f32[32]{0:T(128)S(1)} %div.37), kind=kOutput, calls=%fused_computation.100 | convolution fusion | flops 1612185600 | bytes 23101568 | tf_op jit(solution)/shard_map/dot_general | solution.py:104
  625.9 18.9 %multiply_reduce_fusion = (f32[32]{0:T(128)S(1)}, f32[32,128,128]{2,0,1:T(8,128)}) fusion(f32[32,128,128]{2,0,1:T(8,128)S(1)} %multiply_add_fusion.1, f32[32,128,128]{2,0,1:T(8,128)S(1)} %copy-done.16, f32[32]{0:T(128)S(1)} %div.37, f32[32,256,1]{1,0,2:T(8,128)S(1)} %convolution_bitcast_fusion, f32[128,128]{1,0:T(8,128)S(1)} %copy-done.12, ...), kind=kOutput, calls=%fused_computation.99 | convolution fusion | flops 1622147072 | bytes 8618240 | tf_op jit(solution)/shard_map/dot_general | solution.py:99
  644.8 39.4 %psum.63 = f32[32]{0:T(128)S(1)} all-reduce(f32[32]{0:T(128)S(1)} %get-tuple-element.62), channel_id=1, replica_groups=mesh['row'=8,'col'=4] {'row','col'}, use_global_device_ids=true, to_apply=%region_18.19 | all-reduce | flops 32 | bytes 256 | tf_op jit(solution)/shard_map/psum | solution.py:127
  686.4 2.5 copy.59
  688.9 17.3 %multiply_add_fusion = f32[32,128,128]{2,0,1:T(8,128)S(1)} fusion(f32[32,128,128]{2,0,1:T(8,128)S(1)} %copy-done.18, f32[32,128,128]{2,0,1:T(8,128)S(1)} %copy-done.17, f32[32,256,1]{1,0,2:T(8,128)S(1)} %convolution_bitcast_fusion.2, f32[128,128]{1,0:T(8,128)S(1)} %copy-done.12, s32[128,128]{1,0:T(8,128)S(1)} %copy-done.13, f32[32]{0:T(128)S(1)} %div.38, ...), kind=kOutput, calls=%fused_computation.98 | convolution fusion | flops 1621098496 | bytes 6455552 | tf_op jit(solution)/shard_map/dot_general | solution.py:99
  706.2 2.5 copy.58
  (107 shorter events, 28.3 us)
Async XLA Ops:
  7.2 250.8 %all-reduce.5.cloned.1.call-start = ((), (), s32[]{:S(2)}) async-start(), calls=%async_computation | async-start | bytes 524288 | tf_op jit(solution)/shard_map/psum | solution.py:91
  8.4 40.8 %collective-permute-start = (f32[128,1]{1,0:T(8,128)S(1)}, f32[128,1]{1,0:T(8,128)S(1)}, u32[]{:S(2)}, u32[]{:S(2)}) collective-permute-start(f32[128,1]{1,0:T(8,128)S(1)} %slice.188), channel_id=1, source_target_pairs={{0,1},{1,2},{2,3},{4,5},{5,6},{6,7},{8,9},{9,10},{10,11},{12,13},{... | collective-permute-start | bytes 1544 | tf_op jit(solution)/shard_map/ppermute | solution.py:16
  10.9 14.8 %copy-start.11 = (f32[32,128,128]{2,1,0:T(8,128)S(1)}, f32[32,128,128]{2,1,0:T(8,128)}, u32[]{:S(2)}) copy-start(f32[32,128,128]{2,1,0:T(8,128)} %param.8) | copy-start | bytes 6291460
  10.9 14.8 %copy-start.12 = (f32[128,128]{1,0:T(8,128)S(1)}, f32[128,128]{1,0:T(8,128)}, u32[]{:S(2)}) copy-start(f32[128,128]{1,0:T(8,128)} %param.10) | copy-start | bytes 196612
  10.9 14.8 %copy-start.13 = (s32[128,128]{1,0:T(8,128)S(1)}, s32[128,128]{1,0:T(8,128)}, u32[]{:S(2)}) copy-start(s32[128,128]{1,0:T(8,128)} %param.9) | copy-start | bytes 196612
  11.0 38.2 %collective-permute-start.1 = (f32[1,128]{1,0:T(1,128)S(1)}, f32[1,128]{1,0:T(1,128)S(1)}, u32[]{:S(2)}, u32[]{:S(2)}) collective-permute-start(f32[1,128]{1,0:T(1,128)S(1)} %slice.190), channel_id=1, source_target_pairs={{0,4},{4,8},{8,12},{12,16},{16,20},{20,24},{24,28},{1,5},{5,9},{9,... | collective-permute-start | bytes 1544 | tf_op jit(solution)/shard_map/ppermute | solution.py:16
  20.7 23.2 %copy-start.1 = (f32[256,128,128]{0,2,1:T(8,128)}, f32[256,128,128]{0,2,1:T(8,128)S(1)}, u32[]{:S(2)}) copy-start(f32[256,128,128]{0,2,1:T(8,128)S(1)} %fusion.28) | copy-start | bytes 50331652
  20.8 23.1 %collective-permute-start.2 = (f32[256,1,128]{0,2,1:T(8,128)S(1)}, f32[256,1,128]{0,2,1:T(8,128)S(1)}, u32[]{:S(2)}, u32[]{:S(2)}) collective-permute-start(f32[256,1,128]{0,2,1:T(8,128)S(1)} %get-tuple-element.42), channel_id=1, source_target_pairs={{0,4},{4,8},{8,12},{12,16},{16,20},{20,24},{24,28},{1,5},{5,9},{9,... | collective-permute-start | bytes 393224 | tf_op jit(solution)/shard_map/ppermute | solution.py:26
  24.2 19.5 %copy-start.14 = (s32[128,128]{1,0:T(8,128)S(1)}, s32[128,128]{1,0:T(8,128)}, u32[]{:S(2)}) copy-start(s32[128,128]{1,0:T(8,128)} %param.13) | copy-start | bytes 196612
  24.2 19.5 %copy-start.15 = (f32[8]{0:T(128)S(1)}, f32[8]{0:T(128)}, u32[]{:S(2)}) copy-start(f32[8]{0:T(128)} %param.15) | copy-start | bytes 100
  24.3 19.7 %collective-permute-start.3 = (f32[256,1,128]{0,2,1:T(8,128)S(1)}, f32[256,1,128]{0,2,1:T(8,128)S(1)}, u32[]{:S(2)}, u32[]{:S(2)}) collective-permute-start(f32[256,1,128]{0,2,1:T(8,128)S(1)} %get-tuple-element.41), channel_id=1, source_target_pairs={{4,0},{8,4},{12,8},{16,12},{20,16},{24,20},{28,24},{5,1},{9,5},{13... | collective-permute-start | bytes 393224 | tf_op jit(solution)/shard_map/ppermute | solution.py:27
  44.1 5.2 collective-permute-start.4
  45.4 4.7 collective-permute-start.5
  81.5 5.7 copy-start
  340.7 4.8 collective-permute-start.6
  344.1 5.6 collective-permute-start.7
  355.9 7.7 %collective-permute-start.8 = (f32[32,130,1]{1,0,2:T(8,128)S(1)}, f32[32,130,1]{1,0,2:T(8,128)S(1)}, u32[]{:S(2)}, u32[]{:S(2)}) collective-permute-start(f32[32,130,1]{1,0,2:T(8,128)S(1)} %copy.48), channel_id=1, source_target_pairs={{1,0},{2,1},{3,2},{5,4},{6,5},{7,6},{9,8},{10,9},{11,10},{13,12},{... | collective-permute-start | bytes 49928 | tf_op jit(solution)/shard_map/ppermute | solution.py:27
  360.4 6.8 collective-permute-start.9
  375.4 1.3 copy-start.10
  433.7 17.9 %copy-start.8 = (f32[32,128,128]{2,0,1:T(8,128)S(1)}, f32[32,128,128]{2,0,1:T(8,128)}, u32[]{:S(2)}) copy-start(f32[32,128,128]{2,0,1:T(8,128)} %get-tuple-element.59) | copy-start | bytes 6291460
  451.5 59.9 %copy-start.2 = (f32[32,128,128]{2,0,1:T(8,128)}, f32[32,128,128]{2,0,1:T(8,128)S(1)}, u32[]{:S(2)}) copy-start(f32[32,128,128]{2,0,1:T(8,128)S(1)} %fusion.76) | copy-start | bytes 6291460
  513.9 1.4 copy-start.4
  515.2 5.7 collective-permute-start.10
  519.4 5.6 collective-permute-start.11
  531.2 7.6 %collective-permute-start.12 = (f32[32,130,1]{1,0,2:T(8,128)S(1)}, f32[32,130,1]{1,0,2:T(8,128)S(1)}, u32[]{:S(2)}, u32[]{:S(2)}) collective-permute-start(f32[32,130,1]{1,0,2:T(8,128)S(1)} %copy.53), channel_id=1, source_target_pairs={{1,0},{2,1},{3,2},{5,4},{6,5},{7,6},{9,8},{10,9},{11,10},{13,12},{... | collective-permute-start | bytes 49928 | tf_op jit(solution)/shard_map/ppermute | solution.py:27
  535.7 6.6 collective-permute-start.13
  550.5 16.5 %copy-start.9 = (f32[32,128,128]{2,0,1:T(8,128)}, f32[32,128,128]{2,0,1:T(8,128)S(1)}, u32[]{:S(2)}) copy-start(f32[32,128,128]{2,0,1:T(8,128)S(1)} %fusion.51) | copy-start | bytes 6291460
  550.5 57.5 %copy-start.3 = (f32[32,128,128]{2,0,1:T(8,128)S(1)}, f32[32,128,128]{2,0,1:T(8,128)}, u32[]{:S(2)}) copy-start(f32[32,128,128]{2,0,1:T(8,128)} %copy-done.2) | copy-start | bytes 6291460
  608.0 17.9 %copy-start.5 = (f32[32,128,128]{2,0,1:T(8,128)S(1)}, f32[32,128,128]{2,0,1:T(8,128)}, u32[]{:S(2)}) copy-start(f32[32,128,128]{2,0,1:T(8,128)} %copy-done.4) | copy-start | bytes 6291460
  608.0 17.9 %copy-start.16 = (f32[32,128,128]{2,0,1:T(8,128)S(1)}, f32[32,128,128]{2,0,1:T(8,128)}, u32[]{:S(2)}) copy-start(f32[32,128,128]{2,0,1:T(8,128)} %get-tuple-element.61) | copy-start | bytes 6291460
  625.9 18.9 %copy-start.7 = (f32[32,128,128]{2,0,1:T(8,128)}, f32[32,128,128]{2,0,1:T(8,128)S(1)}, u32[]{:S(2)}) copy-start(f32[32,128,128]{2,0,1:T(8,128)S(1)} %multiply_add_fusion.1) | copy-start | bytes 6291460
  625.9 58.3 %copy-start.6 = (f32[32,128,128]{2,0,1:T(8,128)S(1)}, f32[32,128,128]{2,0,1:T(8,128)}, u32[]{:S(2)}) copy-start(f32[32,128,128]{2,0,1:T(8,128)} %copy-done.4) | copy-start | bytes 6291460
  686.4 2.6 copy-start.17
  686.4 2.6 copy-start.18
Sparse Core Ops, SparseCore 0:
  125.8 132.1 all-reduce.4
where the time goes:
time: 722 us; the launch traced here: 716 us
  blocking collectives  205 us (28%)
  matrix products  203 us (28%)
  other arithmetic  108 us (15%)
  waiting for transfers between devices  96.4 us (13%)
  local copies, waits for them, and re-layouts  51.1 us (7%)
  starting transfers between devices  35.9 us (5%)
  between operations  16.7 us (2%)
    psum x1, waiting for transfers between devices, body(): inverse = invert(lax.psum(partial_matrix, ('row', 'col')))  87.1 us
    psum x2, blocking collectives, refresh(): projected = lax.psum(project(field_image), ('row', 'col'))  81 us
    dot_general x3, matrix products, expand(): jnp.dot(coarse, basis_flat, precision=precise)  56.2 us
    dot_general x3, matrix products, correction_image(): jnp.dot(coarse, image_flat, precision=precise)  54.2 us
    dot_general x3, matrix products, project(): lax.dot_general(field.reshape(load_count, tile_cells), basis_flat, contra...  51 us
    psum x1, blocking collectives, body(): load_sums = lax.psum(project(load_currents), ('row', 'col'))  45.2 us
    sub x3, other arithmetic, stencil(): diagonal * centre - right_link * padded[:, 1:-1, 2:]  40.6 us
    psum x1, blocking collectives, refresh(): weighted_norm = lax.psum(local_norm, ('row', 'col'))  39.8 us
  transfers between devices with their start and end apart: 15, of which 5 were waited for; matrix products, arithmetic and copies ran while one was open for 5% of the time, Pallas kernels for 0%

commit v1 on v0

v1 whole, which is shorter than its diff:
```python
import functools

import jax
import jax.numpy as jnp
from jax import lax
from jax.experimental import pallas as pl
from jax.experimental.pallas import tpu as pltpu
from jax.sharding import PartitionSpec as P

REG = 16
F32 = jnp.float32
precise = lax.Precision.HIGHEST
VM = pl.BlockSpec(memory_space=pltpu.VMEM)
PARAMS = pltpu.CompilerParams(vmem_limit_bytes=56 * 1024 * 1024)


def shape(*dims):
    return jax.ShapeDtypeStruct(dims, F32)


def shifted(value, axis, steps):
    count = lax.axis_size(axis)
    initial, last = (max(0, -steps), min(count, count - steps))
    return lax.ppermute(value, axis, [(i, i + steps) for i in range(initial, last)])


def lookup(entries, classes):
    out = jnp.zeros(classes.shape, F32)
    for k in range(entries.shape[0]):
        out = jnp.where(classes == k, entries[k], out)
    return out


def sweep(size, out_ref):
    lanes = lax.broadcasted_iota(jnp.int32, (size, size), 1)
    rows = lax.broadcasted_iota(jnp.int32, (size, 1), 0)
    row_lanes = lax.broadcasted_iota(jnp.int32, (1, size), 1)

    def step(k, carry):
        matrix = out_ref[...]
        row = out_ref[pl.ds(k, 1), :]
        pivot = jnp.sum(jnp.where(row_lanes == k, row, 0.0), axis=1, keepdims=True)
        col = jnp.sum(jnp.where(lanes == k, matrix, 0.0), axis=1, keepdims=True)
        recip = 1.0 / pivot
        scaled = jnp.where(row_lanes == k, recip, row * recip)
        kept = jnp.where(lanes == k, 0.0, matrix)
        out_ref[...] = kept - jnp.where(rows == k, 0.0, col) * scaled
        out_ref[pl.ds(k, 1), :] = scaled
        return carry

    lax.fori_loop(0, size, step, 0)


BLOCK = 32


def fold(value):
    half = value + pltpu.roll(value, 2 * BLOCK, 1)
    return half + pltpu.roll(half, BLOCK, 1)


def split_dot(exact, value, contract):
    total = None
    for _ in range(3):
        part = value.astype(jnp.bfloat16)
        value = value - part.astype(F32)
        term = lax.dot_general(*((exact, part) if contract[2] else (part, exact)), (contract[:2], ((), ())), preferred_element_type=F32)
        total = term if total is None else total + term
    return total


def pack(hot_ref, sums, dots=()):
    out = None
    for b in (0, 1):
        term = lax.dot_general(hot_ref[b], sums[b], (((1,), (1,)), ((), ())), precision=precise, preferred_element_type=F32)
        out = term if out is None else out + term
    if dots:
        sub = lax.broadcasted_iota(jnp.int32, out.shape, 0)
        ends = jnp.concatenate(list(dots), axis=0)
        full = sums[0].shape[0]
        if ends.shape[0] < full:
            ends = jnp.concatenate([ends, jnp.zeros((full - ends.shape[0], ends.shape[1]), F32)], axis=0)
        total = lax.dot_general(jnp.ones(out.shape[:1] + ends.shape[1:], F32), ends, (((1,), (1,)), ((), ())), precision=precise, preferred_element_type=F32)
        out = jnp.where(sub == out.shape[0] - 1, total, out)
    return out


def unpack(place_ref, gathered):
    block = lax.broadcasted_iota(jnp.int32, gathered.shape, 1) // BLOCK
    stacked = jnp.concatenate([jnp.where(block == k, gathered, 0.0) for k in range(4)], axis=0)
    return fold(split_dot(place_ref[...], stacked, ((1,), (0,), True)))


def gather_kernel(rows, cols, x_ref, out_ref, send_sem, recv_sem):
    count = rows * cols
    me = lax.axis_index("row") * cols + lax.axis_index("col")
    barrier = pltpu.get_barrier_semaphore()

    def target(d):
        other = lax.rem(me + d, count)
        return (other // cols, lax.rem(other, cols))

    def greet(d, carry):
        pl.semaphore_signal(barrier, inc=1, device_id=target(d), device_id_type=pl.DeviceIdType.MESH)
        return carry

    lax.fori_loop(1, count, greet, 0)
    pl.semaphore_wait(barrier, count - 1)

    def copy(d):
        return pltpu.make_async_remote_copy(
            src_ref=x_ref,
            dst_ref=out_ref.at[me],
            send_sem=send_sem.at[d],
            recv_sem=recv_sem.at[d],
            device_id=target(d),
            device_id_type=pl.DeviceIdType.MESH,
        )

    def send(d, carry):
        copy(d).start()
        return carry

    def finish(d, carry):
        copy(d).wait()
        return carry

    lax.fori_loop(1, count, send, 0)
    out_ref[pl.ds(me, 1)] = x_ref[...][None]
    lax.fori_loop(1, count, finish, 0)


def gather(value, ident):
    rows, cols = lax.axis_size("row"), lax.axis_size("col")
    count = rows * cols
    return pl.pallas_call(
        functools.partial(gather_kernel, rows, cols),
        out_shape=shape(count, *value.shape),
        in_specs=[VM],
        out_specs=VM,
        scratch_shapes=[pltpu.SemaphoreType.DMA((count,)), pltpu.SemaphoreType.DMA((count,))],
        compiler_params=pltpu.CompilerParams(collective_id=ident, has_side_effects=True),
    )(value)


def exchange_kernel(rows, cols, *refs):
    sources, landed, (send_sem, recv_sem) = refs[:4], refs[4:8], refs[8:]
    r, c = lax.axis_index("row"), lax.axis_index("col")
    targets = (
        (lax.rem(r + 1, rows), c),
        (lax.rem(r + rows - 1, rows), c),
        (r, lax.rem(c + 1, cols)),
        (r, lax.rem(c + cols - 1, cols)),
    )
    barrier = pltpu.get_barrier_semaphore()
    for target in targets:
        pl.semaphore_signal(barrier, inc=1, device_id=target, device_id_type=pl.DeviceIdType.MESH)
    pl.semaphore_wait(barrier, 4)
    copies = [
        pltpu.make_async_remote_copy(
            src_ref=sources[k],
            dst_ref=landed[k],
            send_sem=send_sem.at[k],
            recv_sem=recv_sem.at[k],
            device_id=targets[k],
            device_id_type=pl.DeviceIdType.MESH,
        )
        for k in range(4)
    ]
    for copy in copies:
        copy.start()
    for copy in copies:
        copy.wait()


def exchange(values, ident):
    return pl.pallas_call(
        functools.partial(exchange_kernel, lax.axis_size("row"), lax.axis_size("col")),
        out_shape=tuple(shape(*v.shape) for v in values),
        in_specs=[VM] * 4,
        out_specs=(VM,) * 4,
        scratch_shapes=[pltpu.SemaphoreType.DMA((4,)), pltpu.SemaphoreType.DMA((4,))],
        compiler_params=pltpu.CompilerParams(collective_id=ident, has_side_effects=True),
    )(*values)


def matrix_kernel(plan, gathered_ref, place_ref, out_ref):
    diagonals = unpack(place_ref, gathered_ref[...])
    size = out_ref.shape[0]
    gap = lax.broadcasted_iota(jnp.int32, (size, size), 1) - lax.broadcasted_iota(jnp.int32, (size, size), 0)
    total = jnp.zeros((size, size), F32)
    for k in range(9):
        total = jnp.where(gap == REG * (k // 3 - 1) + k % 3 - 1, diagonals[:, k : k + 1], total)
    out_ref[...] = total
    sweep(size, out_ref)


def coarse_of(gathered, place_ref, inverse_ref):
    sums = unpack(place_ref, gathered)
    coarse = jnp.dot(inverse_ref[...], sums, precision=precise, preferred_element_type=F32)
    return sums, coarse


def expand_into(out_ref, coarse, expand_ref):
    near = split_dot(expand_ref[...], coarse, ((0,), (0,), False))
    loads = BLOCK
    cols = out_ref.shape[-1]
    levels = out_ref.shape[1] // loads
    for b in (0, 1):
        for l in range(levels):
            k = b * levels + l
            out_ref[b, l * loads : (l + 1) * loads, :] = near[:loads, k * cols : (k + 1) * cols]


def wide(value):
    return jnp.broadcast_to(value, (value.shape[1],) * 2).T[:BLOCK]


def totals(gathered_ref, count):
    summed = jnp.sum(gathered_ref[...].reshape(-1, 8, gathered_ref.shape[-1]), axis=0)[7:8]
    block = lax.broadcasted_iota(jnp.int32, summed.shape, 1) // BLOCK
    return [fold(jnp.where(block == k, summed, 0.0)) for k in range(count)]


def solve_first(plan, gathered_ref, place_ref, inverse_ref, expand_ref, cx_ref, c_ref):
    _, coarse = coarse_of(gathered_ref[...], place_ref, inverse_ref)
    c_ref[...] = coarse
    expand_into(cx_ref, coarse, expand_ref)


def solve_second(plan, gathered_ref, place_ref, inverse_ref, expand_ref, cx_ref, c_ref, scal_ref, alpha_ref):
    sums, coarse = coarse_of(gathered_ref[...], place_ref, inverse_ref)
    rho, image_dot = totals(gathered_ref, 2)
    curve = image_dot - jnp.sum(coarse * sums, axis=0, keepdims=True)
    alpha = rho / curve
    c_ref[...] = coarse
    scal_ref[0:1] = rho
    scal_ref[1:2] = curve
    scal_ref[2:3] = alpha
    alpha_ref[...] = wide(alpha)
    expand_into(cx_ref, coarse, expand_ref)


def solve_third(plan, gathered_ref, place_ref, inverse_ref, expand_ref, c0_ref, c1_ref, scal_ref, cs_ref, cx_ref, out_ref):
    sums, coarse = coarse_of(gathered_ref[...], place_ref, inverse_ref)
    rho1, qz, image_dot = totals(gathered_ref, 3)
    rho, curve, alpha0 = scal_ref[0:1], scal_ref[1:2], scal_ref[2:3]
    beta = rho1 / rho
    curve1 = image_dot - jnp.sum(coarse * sums, axis=0, keepdims=True) + 2.0 * beta * qz + beta * beta * curve
    alpha1 = rho1 / curve1
    mix = alpha0 + alpha1 * beta
    expand_into(cx_ref, coarse, expand_ref)
    expand_into(cs_ref, c0_ref[...] - alpha1 * coarse - mix * c1_ref[...], expand_ref)
    out_ref[0] = wide(mix)
    out_ref[1] = wide(alpha1)
    out_ref[2] = wide(beta)


class Plan:
    def __init__(self, rows, loads, height):
        self.rows, self.loads, self.height = rows, loads, height
        self.parts = rows // height + 1
        self.levels = self.parts + 1

    def chunks(self):
        half = self.height // 2
        for part in range(self.parts):
            yield part, max(0, part * self.height - half), min(self.rows, part * self.height + half)


def over_rows(first, last, step, init, group=4):
    def body(g, carry):
        for u in range(group):
            carry = step(first + g * group + u, carry)
        return carry

    return lax.fori_loop(0, (last - first) // group, body, init)


def row_of(ref, k, i):
    return ref[k, pl.ds(i, 1), :]


def spread(mask_ref, cx, i):
    out = row_of(mask_ref, 0, i) * cx[0]
    for k in range(1, 4):
        out = out + row_of(mask_ref, k, i) * cx[k]
    return out


def expansions(plan, cx_ref, part):
    n = plan.loads
    return [cx_ref[b, (part + a) * n : (part + a + 1) * n, :] for a in (0, 1) for b in (0, 1)]


def sums_kernel(plan, b_ref, mask_ref, image_ref, hot_ref, out_ref, s_ref, pair_ref):
    n = plan.loads
    s_ref[...] = jnp.zeros_like(s_ref)
    for part, first, last in plan.chunks():
        def step(i, acc):
            v = b_ref[pl.ds(i, n, stride=plan.rows), :]
            return tuple(x + row_of(mask_ref, k, i) * v for k, x in enumerate(acc))

        acc = over_rows(first, last, step, (jnp.zeros((n, s_ref.shape[-1]), F32),) * 4)
        add_sums(plan, s_ref, part, acc)
    out_ref[0] = pack(hot_ref, s_ref)
    pair_ref[...] = jnp.zeros_like(pair_ref)
    for part, first, last in plan.chunks():
        for k in range(4):
            for m in range(4):
                da, db = m // 2 - k // 2, m % 2 - k % 2
                at = (part + k // 2) * BLOCK + (da + 1) * 3 + db + 1
                term = jnp.sum(mask_ref[k, first:last, :] * image_ref[m, first:last, :], axis=0, keepdims=True)
                pair_ref[k % 2, at : at + 1, :] = pair_ref[k % 2, at : at + 1, :] + term
    out_ref[1] = pack(hot_ref, pair_ref)


def add_sums(plan, s_ref, part, acc):
    n = plan.loads
    for a in (0, 1):
        for b in (0, 1):
            where = slice((part + a) * n, (part + a + 1) * n)
            s_ref[b, where, :] = s_ref[b, where, :] + acc[2 * a + b]


def pack_edges(edges, z, i, cols):
    left, right = edges
    lane = lax.broadcasted_iota(jnp.int32, z.shape, 1)
    left = jnp.where(lane == i, pltpu.roll(z, i, 1), left)
    right = jnp.where(lane == i, pltpu.roll(z, lax.rem(i + 1, z.shape[1]), 1), right)
    return left, right


def first_kernel(plan, b_ref, image_ref, coef_ref, cx_ref, r_ref, z_ref, rho_ref, edge_ref):
    n = plan.loads
    zero = jnp.zeros((n, b_ref.shape[-1]), F32)
    carry = (zero, zero, zero)
    for part, first, last in plan.chunks():
        cx = expansions(plan, cx_ref, part)

        def step(i, carry):
            rho, *edges = carry
            r = b_ref[pl.ds(i, n, stride=plan.rows), :] - spread(image_ref, cx, i)
            z = r / row_of(coef_ref, 0, i)
            at = pl.ds(pl.multiple_of(i * n, n), n)
            r_ref[at, :] = r
            z_ref[at, :] = z
            return (rho + r * z, *pack_edges(edges, z, i, z.shape[1]))

        carry = over_rows(first, last, step, carry)
    rho_ref[0] = carry[0]
    edge_ref[0] = carry[1]
    edge_ref[1] = carry[2]


def image_kernel(plan, z_ref, above_ref, below_ref, left_ref, right_ref, coef_ref, mask_ref, hot_ref, dots_ref, f_ref, out_ref, s_ref):
    n = plan.loads
    cols = z_ref.shape[-1]
    zero = jnp.zeros((n, cols), F32)
    lane = lax.broadcasted_iota(jnp.int32, (n, cols), 1)
    s_ref[...] = jnp.zeros_like(s_ref)
    left_pack, right_pack = left_ref[...], right_ref[...]

    def image(i, z, up, down):
        before = jnp.where(lane == 0, pltpu.roll(left_pack, lax.rem(cols - i, cols), 1), pltpu.roll(z, 1, 1))
        after = jnp.where(lane == cols - 1, pltpu.roll(right_pack, cols - 1 - i, 1), pltpu.roll(z, cols - 1, 1))
        return (
            row_of(coef_ref, 0, i) * z
            - row_of(coef_ref, 1, i) * after
            - row_of(coef_ref, 2, i) * before
            - row_of(coef_ref, 3, i) * down
            - row_of(coef_ref, 4, i) * up
        )

    def load(i):
        return z_ref[pl.ds(pl.multiple_of(i * n, n), n), :]

    def step(i, carry):
        return finish(i, load(i), load(i - 1), load(i + 1), carry)

    def finish(i, z, up, down, carry):
        f = image(i, z, up, down)
        f_ref[pl.ds(pl.multiple_of(i * n, n), n), :] = f
        zf, *acc = carry
        return (zf + z * f, *[x + row_of(mask_ref, k, i) * f for k, x in enumerate(acc)])

    zf = zero
    for part, first, last in plan.chunks():
        carry = (zf,) + (zero,) * 4
        low, high = first, last
        if first == 0:
            carry = finish(0, load(0), above_ref[...], load(1), carry)
            low = 1
        if last == plan.rows:
            high = last - 1
        carry = over_rows(low, high, step, carry, 1 if (high - low) % 4 else 4)
        if last == plan.rows:
            carry = finish(last - 1, load(last - 1), load(last - 2), below_ref[...], carry)
        zf, *acc = carry
        add_sums(plan, s_ref, part, acc)
    out_ref[...] = pack(hot_ref, s_ref, [dots_ref[k] for k in range(dots_ref.shape[0])] + [zf])


def second_kernel(plan, r_ref, f_ref, image_ref, coef_ref, cx_ref, alpha_ref, r1_ref, z1_ref, q_ref, dots_ref, edge_ref):
    n = plan.loads
    zero = jnp.zeros((n, r_ref.shape[-1]), F32)
    carry = (zero,) * 4
    alpha = alpha_ref[...]
    for part, first, last in plan.chunks():
        cx = expansions(plan, cx_ref, part)

        def step(i, carry):
            rho, qz, *edges = carry
            at = pl.ds(pl.multiple_of(i * n, n), n)
            q = f_ref[at, :] - spread(image_ref, cx, i)
            r = r_ref[at, :] - alpha * q
            z = r / row_of(coef_ref, 0, i)
            q_ref[at, :] = q
            r1_ref[at, :] = r
            z1_ref[at, :] = z
            return (rho + r * z, qz + q * z, *pack_edges(edges, z, i, z.shape[1]))

        carry = over_rows(first, last, step, carry)
    dots_ref[0] = carry[0]
    dots_ref[1] = carry[1]
    edge_ref[0] = carry[2]
    edge_ref[1] = carry[3]


def last_kernel(plan, z_ref, z1_ref, r1_ref, f1_ref, q_ref, mask_ref, image_ref, cs_ref, cx_ref, scal_ref, s_out, r_out):
    n = plan.loads
    mix, alpha, beta = scal_ref[0], scal_ref[1], scal_ref[2]
    for part, first, last in plan.chunks():
        cs = expansions(plan, cs_ref, part)
        cx = expansions(plan, cx_ref, part)

        def step(i, carry):
            at = pl.ds(pl.multiple_of(i * n, n), n)
            to = pl.ds(i, n, stride=plan.rows)
            s_out[to, :] = spread(mask_ref, cs, i) + mix * z_ref[at, :] + alpha * z1_ref[at, :]
            q1 = f1_ref[at, :] - spread(image_ref, cx, i) + beta * q_ref[at, :]
            r_out[to, :] = r1_ref[at, :] - alpha * q1
            return carry

        over_rows(first, last, step, 0, 2)


def body(load_currents, labels, bump_height, horizontal_class, vertical_class, pad_class, edge_table, pad_table):
    rows, cols = labels.shape
    loads = load_currents.shape[0]
    regions = REG * REG
    grid_rows = lax.axis_size("row") * rows
    grid_cols = lax.axis_size("col") * cols
    height, width = grid_rows // REG, grid_cols // REG
    plan = Plan(rows, loads, height)
    levels = plan.levels
    ri, ci = lax.axis_index("row"), lax.axis_index("col")
    row_ids = ri * rows + lax.broadcasted_iota(jnp.int32, (rows, cols), 0)
    col_ids = ci * cols + lax.broadcasted_iota(jnp.int32, (rows, cols), 1)
    right_link = jnp.where(col_ids == grid_cols - 1, 0.0, lookup(edge_table, horizontal_class))
    down_link = jnp.where(row_ids == grid_rows - 1, 0.0, lookup(edge_table, vertical_class))
    named = labels.astype(F32)
    right_end = jnp.stack([named[:, -1], bump_height[:, -1], right_link[:, -1]])
    left_end = jnp.stack([named[:, 0], bump_height[:, 0]])
    low_end = jnp.stack([named[-1], bump_height[-1], down_link[-1]])
    top_end = jnp.stack([named[0], bump_height[0]])
    before = shifted(right_end, "col", 1)
    after = shifted(left_end, "col", -1)
    above = shifted(low_end, "row", 1)
    below = shifted(top_end, "row", -1)

    def at_left(value, k):
        return jnp.concatenate([before[k][:, None], value[:, :-1]], axis=1)

    def at_right(value, k):
        return jnp.concatenate([value[:, 1:], after[k][:, None]], axis=1)

    def at_top(value, k):
        return jnp.concatenate([above[k][None], value[:-1]], axis=0)

    def at_low(value, k):
        return jnp.concatenate([value[1:], below[k][None]], axis=0)

    left_link = at_left(right_link, 2)
    upper_link = at_top(down_link, 2)
    diagonal = lookup(pad_table, pad_class) + right_link + left_link + down_link + upper_link
    base_row = (row_ids + height // 2) // height - 1
    base_col = (col_ids + width // 2) // width - 1

    def masks(name, weight):
        name = name.astype(jnp.int32)
        a, b = name // REG - base_row, name % REG - base_col
        return jnp.stack([jnp.where((a == i) & (b == j), weight, 0.0) for i in (0, 1) for j in (0, 1)])

    mask = masks(named, bump_height)
    image = (
        masks(named, diagonal * bump_height)
        - masks(at_right(named, 0), right_link * at_right(bump_height, 1))
        - masks(at_left(named, 0), left_link * at_left(bump_height, 1))
        - masks(at_low(named, 0), down_link * at_low(bump_height, 1))
        - masks(at_top(named, 0), upper_link * at_top(bump_height, 1))
    )
    coef = jnp.stack([diagonal, right_link, left_link, down_link, upper_link])

    span = cols // width + 2
    lane_base = (lax.iota(jnp.int32, cols) + width // 2) // width
    hot = jnp.stack([(lane_base[None] + b == lax.iota(jnp.int32, 8)[:, None]).astype(F32) for b in (0, 1)])
    count = lax.axis_size("row") * lax.axis_size("col")
    here = lax.broadcasted_iota(jnp.int32, (regions, 4 * count * 8), 0)
    sent = lax.broadcasted_iota(jnp.int32, (regions, 4 * count * 8), 1)
    level, device, x = sent // (count * 8), sent // 8 % count, sent % 8
    at_row = device // lax.axis_size("col") * (rows // height) - 1 + level
    at_col = device % lax.axis_size("col") * (cols // width) - 1 + x
    place = ((here // REG == at_row) & (here % REG == at_col) & (x < span) & (level < levels)).astype(jnp.bfloat16)
    here = lax.broadcasted_iota(jnp.int32, (regions, 2 * levels * cols), 0)
    lane = lax.broadcasted_iota(jnp.int32, (regions, 2 * levels * cols), 1)
    which, lane = lane // cols, lane % cols
    at_row = ri * (rows // height) - 1 + which % levels
    at_col = ci * (cols // width) - 1 + (lane + width // 2) // width + which // levels
    expand = ((here // REG == at_row) & (here % REG == at_col)).astype(jnp.bfloat16)

    def call(kernel, outs, *args, scratch=()):
        return pl.pallas_call(
            functools.partial(kernel, plan),
            out_shape=outs,
            in_specs=[VM] * len(args),
            out_specs=jax.tree.map(lambda _: VM, outs),
            scratch_shapes=scratch,
            compiler_params=PARAMS,
        )(*args)

    s_shape = shape(2, levels * loads, cols)
    sums_scratch = [pltpu.VMEM((2, 4 * BLOCK, cols), F32)]
    field = shape(rows * loads, cols)
    message = shape(8, 4 * BLOCK)
    coarse_shape = shape(regions, 4 * BLOCK)

    def image_of(z, edges, dots, ident):
        landed = exchange((z[-loads:], z[:loads], edges[1], edges[0]), ident)
        f, sums = call(image_kernel, (field, message), z, *landed, coef, mask, hot, dots, scratch=sums_scratch)
        return f, gather(sums, ident + 1).reshape(count * 8, 4 * BLOCK)

    flat = load_currents.reshape(loads * rows, cols)
    first = call(sums_kernel, shape(2, 8, 4 * BLOCK), flat, mask, image, hot, scratch=sums_scratch * 2)
    first = gather(first, 0)
    inverse = call(matrix_kernel, shape(regions, regions), first[:, 1].reshape(count * 8, 4 * BLOCK), place)
    cx, c0 = call(solve_first, (s_shape, coarse_shape), first[:, 0].reshape(count * 8, 4 * BLOCK), place, inverse, expand)
    r0, z0, rho_lanes, edges = call(
        first_kernel, (field, field, shape(1, loads, cols), shape(2, loads, cols)), flat, image, coef, cx
    )
    f0, sums = image_of(z0, edges, rho_lanes, 1)
    cx, c1, scal, alpha = call(
        solve_second, (s_shape, coarse_shape, shape(8, 4 * BLOCK), shape(loads, cols)), sums, place, inverse, expand
    )
    r1, z1, q0, dots, edges = call(
        second_kernel,
        (field, field, field, shape(2, loads, cols), shape(2, loads, cols)),
        r0, f0, image, coef, cx, alpha,
    )
    f1, sums = image_of(z1, edges, dots, 3)
    cs, cx, scal = call(
        solve_third, (s_shape, s_shape, shape(3, loads, cols)), sums, place, inverse, expand, c0, c1, scal
    )
    s, r = call(
        last_kernel, (shape(loads * rows, cols),) * 2,
        z0, z1, r1, f1, q0, mask, image, cs, cx, scal,
    )
    return (s.reshape(load_currents.shape), r.reshape(load_currents.shape))


def solution(mesh):
    grid = P("row", "col")
    cube = P(None, "row", "col")
    return jax.shard_map(
        body,
        mesh=mesh,
        in_specs=(cube, grid, grid, grid, grid, grid, P(), P()),
        out_specs=(cube, cube),
        check_vma=False,
    )
```

time: 722 us -> 207 us (0.29)
  blocking collectives: 205 us -> 0 us
  matrix products: 203 us -> 0 us
  Pallas kernels: 0 us -> 156 us
  waiting for transfers between devices: 96.4 us -> 0.42 us
  other arithmetic: 108 us -> 21.6 us
  local copies, waits for them, and re-layouts: 51.1 us -> 15.3 us
  starting transfers between devices: 35.9 us -> 11.1 us
  between operations: 16.7 us -> 1.15 us
    psum x5 -> x0, blocking collectives: 205 us -> none  [the longest x2 81 us: refresh(): projected = lax.psum(project(field_image), ('row', 'col'))]
    dot_general x13 -> x0, matrix products: 201 us -> none  [the longest x3 56.2 us: expand(): jnp.dot(coarse, basis_flat, precision=precise)]
    pallas_call x0 -> x15, Pallas kernels: none -> 156 us  [the longest x10 104 us: call(): pl.pallas_call(functools.partial(kernel, plan), out_shape=outs, in_specs=...]
    psum x1 -> x0, waiting for transfers between devices: 87.1 us -> none  [body(): inverse = invert(lax.psum(partial_matrix, ('row', 'col')))]
    another operation x9 -> x15, other arithmetic: 54.1 us -> 11.9 us  [the longest x9 11.2 us: masks(): jnp.stack([jnp.where((a == i) & (b == j), weight, 0.0) for i in (0, 1) fo...]
    sub x4 -> x2, other arithmetic: 42.7 us -> 0.82 us  [the longest x1 0.81 us: body(): masks(named, diagonal * bump_height)]
    ppermute x14 -> x4, starting transfers between devices: 35.8 us -> 11.1 us  [shifted(): lax.ppermute(value, axis, [(i, i + steps) for i in range(initial, last)])]
    ppermute x4 -> x0, local copies, waits for them, and re-layouts: 14.3 us -> none  [the longest x2 7.18 us: extended(): before = lax.ppermute(last, axis, up)]
  transfers between devices with their start and end apart: 15 -> 4, of which waited for: 5 -> 1; matrix products, arithmetic and copies ran while one was open for 5% -> 10% of each run, Pallas kernels for 0% -> 0%
where the time goes in v1:
time: 207 us; the launch traced here: 206 us
  Pallas kernels  156 us (75%)
  other arithmetic  21.6 us (10%)
  local copies, waits for them, and re-layouts  15.3 us (7%)
  starting transfers between devices  11.1 us (5%)
    pallas_call x10, Pallas kernels, call(): pl.pallas_call(functools.partial(kernel, plan), out_shape=outs, in_specs=...  104 us
    pallas_call x3, Pallas kernels, gather(): pl.pallas_call(functools.partial(gather_kernel, rows, cols), out_shape=sh...  34.1 us
    pallas_call x2, Pallas kernels, exchange(): pl.pallas_call(functools.partial(exchange_kernel, lax.axis_size('row'), l...  18.4 us
    another operation x9, other arithmetic, masks(): jnp.stack([jnp.where((a == i) & (b == j), weight, 0.0) for i in (0, 1) fo...  11.2 us
    ppermute x4, starting transfers between devices, shifted(): lax.ppermute(value, axis, [(i, i + steps) for i in range(initial, last)])  11.1 us
    unnamed x2, other arithmetic  5.05 us
  transfers between devices with their start and end apart: 4, of which 1 were waited for; matrix products, arithmetic and copies ran while one was open for 10% of the time, Pallas kernels for 0%

profile of v1, /device:TPU:0, one launch (start us, length us, event | category | flops | bytes accessed | tf_op | source)
XLA Modules:
  0.0 205.8 jit_solution(16291849451187427622)
XLA Ops:
  0.6 0.9 convert_element_type.85
  1.5 0.7 fusion.86
  2.2 1.3 collective-permute-start.3
  3.5 1.1 slice_reduce_fusion.3
  4.6 0.2 slice_reduce_fusion
  4.8 1.3 collective-permute-start.2
  6.5 1.0 slice_bitcast_fusion.5
  7.5 0.9 slice_bitcast_fusion.2
  8.4 1.6 fusion.90
  10.1 1.6 fusion.89
  11.7 0.6 add_convert_fusion.hot_ref
  12.3 1.2 fusion.16.expand_ref
  13.5 1.2 fusion.19.place_ref
  14.7 0.1 copy.18
  14.8 0.1 copy.17
  15.0 5.0 %select_bitcast_fusion.11 = (f32[1,128,128]{2,1,0:T(8,128)S(1)}, pred[128,128]{1,0:T(8,128)(4,1)S(1)}, pred[128,128]{1,0:T(8,128)(4,1)S(1)}, s32[128,128]{1,0:T(...) fusion(s32[128]{0:T(128)S(1)} %get-tuple-element.193, ...), kind=kLoop, calls=%fused_computation.160 | loop fusion | flops 1146880 | bytes 559776 | tf_op jit(solution)/shard_map/stack | solution.py:493
  20.0 0.2 slice_reduce_fusion.1
  20.2 3.0 %collective-permute-start = (f32[3,128]{1,0:T(4,128)S(1)}, f32[3,128]{1,0:T(4,128)S(1)}, u32[]{:S(2)}, u32[]{:S(2)}) collective-permute-start(f32[3,128]{1,0:T(4,128)S(1)} %pad_maximum_fusion.3), channel_id=1, source_target_pairs={{0,1},{1,2},{2,3},{4,5},{5,6},{6,7},{8,9},{9,10},{10,11},{12,13},{... | collective-permute-start | bytes 4616 | tf_op jit(solution)/shard_map/ppermute | solution.py:24
  23.3 5.0 %select_bitcast_fusion.7 = (f32[1,128,128]{2,1,0:T(8,128)S(1)}, pred[128,128]{1,0:T(8,128)(4,1)S(1)}, s32[128,128]{1,0:T(8,128)S(1)}, f32[128,128]{1,0:T(8,128)S(1)}, f32[128,128]{1,0:T(8,128)S(1)}) fusion(s32[128]{0:T(128)S(1)} %get-tuple-element.193, s32[128]{0:T(128)S(1)} %get-tuple-element.194, pred[128]{0:T(512)(128)(4,1)S(1)} %get-tuple-element.192, ...), kind=kLoop, calls=%fused_computation.153 | loop fusion | flops 1146880 | bytes 477856 | tf_op jit(solution)/shard_map/stack | solution.py:493
  28.3 5.5 %collective-permute-start.1 = (f32[3,128]{1,0:T(4,128)S(1)}, f32[3,128]{1,0:T(4,128)S(1)}, u32[]{:S(2)}, u32[]{:S(2)}) collective-permute-start(f32[3,128]{1,0:T(4,128)S(1)} %pad_maximum_fusion.4), channel_id=1, source_target_pairs={{0,4},{4,8},{8,12},{12,16},{16,20},{20,24},{24,28},{1,5},{5,9},{9,... | collective-permute-start | bytes 4616 | tf_op jit(solution)/shard_map/ppermute | solution.py:24
  33.9 0.2 select_bitcast_fusion.3
  34.3 0.1 copy.20
  34.7 0.4 collective-permute-done.1
  35.1 5.0 %bitcast_dynamic-update-slice_fusion.4 = (f32[5,128,128]{2,1,0:T(8,128)S(1)}, f32[128,128]{1,0:T(8,128)S(1)}) fusion(f32[127,128]{1,0:T(8,128)S(1)} %get-tuple-element.138, f32[1,128]{1,0:T(1,128)S(1)} %get-tuple-element.165, f32[128,128]{1,0:T(8,128)S(1)} %get-tuple-element.95, f32[128,127]{1,0:T(8,128)S(1)} %get-tuple-element.146, f32[128,1]{1,0:T(8,128)S(1)} %copy.16, ...), kind=kLoop, calls=%fused_computation.143 | loop fusion | flops 360447 | bytes 458784
  40.3 0.2 and_select_fusion.7
  40.6 0.2 and_select_fusion.3
  40.9 0.7 pad_maximum_fusion.mask_ref
  41.6 0.8 fusion.23.image_ref
  42.5 4.5 %shard_map.95.x_ref = f32[2,8,128]{2,1,0:T(8,128)} custom-call(f32[4096,128]{1,0:T(8,128)} %bitcast.110, f32[4,128,128]{2,1,0:T(8,128)} %pad_maximum_fusion.mask_ref, f32[4,128,128]{2,1,0:T(8,128)} %fusion.23.image_ref, f32[2,8,128]{2,1,0:T(8,128)} %add_convert_fusion.hot_ref), custom_call_target="tpu_custom_call" | custom-call | tf_op jit(solution)/shard_map/pallas_call | solution.py:523
  47.0 14.7 %shard_map.96 = f32[32,2,8,128]{3,2,1,0:T(8,128)} custom-call(f32[2,8,128]{2,1,0:T(8,128)} %shard_map.95.x_ref), custom_call_target="tpu_custom_call" | custom-call | tf_op jit(solution)/shard_map/pallas_call | solution.py:136
  61.7 1.7 slice_bitcast_fusion
  63.4 36.5 %shard_map.97.inverse_ref = f32[256,256]{1,0:T(8,128)} custom-call(f32[256,128]{1,0:T(8,128)} %get-tuple-element.125.gathered_ref, bf16[256,1024]{1,0:T(8,128)(2,1)} %fusion.19.place_ref), custom_call_target="tpu_custom_call" | custom-call | tf_op jit(solution)/shard_map/pallas_call | solution.py:523
  99.9 3.8 %shard_map.98 = (f32[2,128,128]{2,1,0:T(8,128)}, f32[256,128]{1,0:T(8,128)}) custom-call(f32[256,128]{1,0:T(8,128)} %get-tuple-element.126.gathered_ref, bf16[256,1024]{1,0:T(8,128)(2,1)} %fusion.19.place_ref, f32[256,256]{1,0:T(8,128)} %shard_map.97.inverse_ref, bf16[256,1024]{1,0:T(8,128)(2,1)} %fusion.16.expand_ref), custom_call_target="tpu_custom_call" | custom-call | tf_op jit(solution)/shard_map/pallas_call | solution.py:523
  103.7 8.0 %shard_map.99 = (f32[4096,128]{1,0:T(8,128)}, f32[4096,128]{1,0:T(8,128)}, f32[1,32,128]{2,1,0:T(8,128)}, f32[2,32,128]{2,1,0:T(8,128)}) custom-call(f32[4096,128]{1,0:T(8,128)} %bitcast.111, f32[4,128,128]{2,1,0:T(8,128)} %fusion.23.image_ref, f32[5,128,128]{2,1,0:T(8,128)} %copy-done, f32[2,128,128]{2,1,0:T(8,128)} %get-tuple-element.34.cx_ref), custom_call_target="tpu_custom_call" | custom-call | tf_op jit(solution)/shard_map/pallas_call | solution.py:523
  111.6 1.3 slice_bitcast_fusion.8
  113.0 1.3 fusion.85
  114.3 9.6 %shard_map.100 = (f32[32,128]{1,0:T(8,128)}, f32[32,128]{1,0:T(8,128)}, f32[32,128]{1,0:T(8,128)}, f32[32,128]{1,0:T(8,128)}) custom-call(f32[32,128]{1,0:T(8,128)} %get-tuple-element.124.refs_0_, f32[32,128]{1,0:T(8,128)} %get-tuple-element.123.refs_1_, f32[32,128]{1,0:T(8,128)} %get-tuple-element.161.refs_2_, f32[32,128]{1,0:T(8,128)} %get-tuple-element.160.refs_3_), custom_call_target="tpu_custom_call" | custom-call | tf_op jit(solution)/shard_map/pallas_call | solution.py:177
  123.9 11.7 %shard_map.101 = (f32[4096,128]{1,0:T(8,128)}, f32[8,128]{1,0:T(8,128)}) custom-call(f32[4096,128]{1,0:T(8,128)} %get-tuple-element.35.z_ref, f32[32,128]{1,0:T(8,128)} %get-tuple-element.38.above_ref, f32[32,128]{1,0:T(8,128)} %get-tuple-element.39.below_ref, f32[32,128]{1,0:T(8,128)} %get-tuple-element.40.left_ref, f32[32,128]{1,0:T(8,128)} %get-tuple-element.41.right_ref, ...), custom_call_target="tpu_custom_call" | custom-call | tf_op jit(solution)/shard_map/pallas_call | solution.py:523
  135.6 9.7 %shard_map.102 = f32[32,8,128]{2,1,0:T(8,128)} custom-call(f32[8,128]{1,0:T(8,128)} %get-tuple-element.44.x_ref), custom_call_target="tpu_custom_call" | custom-call | tf_op jit(solution)/shard_map/pallas_call | solution.py:136
  145.3 3.8 %shard_map.103 = (f32[2,128,128]{2,1,0:T(8,128)}, f32[256,128]{1,0:T(8,128)}, f32[8,128]{1,0:T(8,128)}, f32[32,128]{1,0:T(8,128)}) custom-call(f32[256,128]{1,0:T(8,128)} %bitcast.113, bf16[256,1024]{1,0:T(8,128)(2,1)} %fusion.19.place_ref, f32[256,256]{1,0:T(8,128)} %shard_map.97.inverse_ref, bf16[256,1024]{1,0:T(8,128)(2,1)} %fusion.16.expand_ref), custom_call_target="tpu_custom_call" | custom-call | tf_op jit(solution)/shard_map/pallas_call | solution.py:523
  149.1 8.6 %shard_map.104 = (f32[4096,128]{1,0:T(8,128)}, f32[4096,128]{1,0:T(8,128)}, f32[4096,128]{1,0:T(8,128)}, f32[2,32,128]{2,1,0:T(8,128)}, f32[2,32,128]{2,1,0:T(8,128)}) custom-call(f32[4096,128]{1,0:T(8,128)} %get-tuple-element.36.r_ref, f32[4096,128]{1,0:T(8,128)} %get-tuple-element.43.f_ref, f32[4,128,128]{2,1,0:T(8,128)} %fusion.23.image_ref, ...), custom_call_target="tpu_custom_call" | custom-call | tf_op jit(solution)/shard_map/pallas_call | solution.py:523
  157.7 1.3 slice_bitcast_fusion.6
  159.0 1.3 fusion.84
  160.4 8.8 %shard_map.105 = (f32[32,128]{1,0:T(8,128)}, f32[32,128]{1,0:T(8,128)}, f32[32,128]{1,0:T(8,128)}, f32[32,128]{1,0:T(8,128)}) custom-call(f32[32,128]{1,0:T(8,128)} %get-tuple-element.122.refs_0_, f32[32,128]{1,0:T(8,128)} %get-tuple-element.121.refs_1_, f32[32,128]{1,0:T(8,128)} %get-tuple-element.159.refs_2_, f32[32,128]{1,0:T(8,128)} %get-tuple-element.158.refs_3_), custom_call_target="tpu_custom_call" | custom-call | tf_op jit(solution)/shard_map/pallas_call | solution.py:177
  169.2 11.7 %shard_map.106 = (f32[4096,128]{1,0:T(8,128)}, f32[8,128]{1,0:T(8,128)}) custom-call(f32[4096,128]{1,0:T(8,128)} %get-tuple-element.47.z_ref.z1_ref, f32[32,128]{1,0:T(8,128)} %get-tuple-element.50.above_ref, f32[32,128]{1,0:T(8,128)} %get-tuple-element.51.below_ref, f32[32,128]{1,0:T(8,128)} %get-tuple-element.52.left_ref, ...), custom_call_target="tpu_custom_call" | custom-call | tf_op jit(solution)/shard_map/pallas_call | solution.py:523
  180.9 9.7 %shard_map.107 = f32[32,8,128]{2,1,0:T(8,128)} custom-call(f32[8,128]{1,0:T(8,128)} %get-tuple-element.57.x_ref), custom_call_target="tpu_custom_call" | custom-call | tf_op jit(solution)/shard_map/pallas_call | solution.py:136
  190.6 4.1 %shard_map.108 = (f32[2,128,128]{2,1,0:T(8,128)}, f32[2,128,128]{2,1,0:T(8,128)}, f32[3,32,128]{2,1,0:T(8,128)}) custom-call(f32[256,128]{1,0:T(8,128)} %bitcast.112, bf16[256,1024]{1,0:T(8,128)(2,1)} %fusion.19.place_ref, f32[256,256]{1,0:T(8,128)} %shard_map.97.inverse_ref, bf16[256,1024]{1,0:T(8,128)(2,1)} %fusion.16.expand_ref, ...), custom_call_target="tpu_custom_call" | custom-call | tf_op jit(solution)/shard_map/pallas_call | solution.py:523
  194.6 11.1 %shard_map.109 = (f32[4096,128]{1,0:T(8,128)}, f32[4096,128]{1,0:T(8,128)}) custom-call(f32[4096,128]{1,0:T(8,128)} %get-tuple-element.35.z_ref, f32[4096,128]{1,0:T(8,128)} %get-tuple-element.47.z_ref.z1_ref, f32[4096,128]{1,0:T(8,128)} %get-tuple-element.48.r1_ref, f32[4096,128]{1,0:T(8,128)} %get-tuple-element.55.f1_ref, ...), custom_call_target="tpu_custom_call" | custom-call | tf_op jit(solution)/shard_map/pallas_call | solution.py:523
  (63 shorter events, 1.1 us)
Async XLA Ops:
  0.6 14.3 %copy-start.3 = (s32[128,128]{1,0:T(8,128)S(1)}, s32[128,128]{1,0:T(8,128)}, u32[]{:S(2)}) copy-start(s32[128,128]{1,0:T(8,128)} %param.11) | copy-start | bytes 196612
  0.6 22.6 %copy-start.4 = (s32[128,128]{1,0:T(8,128)S(1)}, s32[128,128]{1,0:T(8,128)}, u32[]{:S(2)}) copy-start(s32[128,128]{1,0:T(8,128)} %param.12) | copy-start | bytes 196612
  2.2 21.0 %collective-permute-start.3 = (f32[2,128]{1,0:T(2,128)S(1)}, f32[2,128]{1,0:T(2,128)S(1)}, u32[]{:S(2)}, u32[]{:S(2)}) collective-permute-start(f32[2,128]{1,0:T(2,128)S(1)} %pad_maximum_fusion.6), channel_id=1, source_target_pairs={{4,0},{8,4},{12,8},{16,12},{20,16},{24,20},{28,24},{5,1},{9,5},{13... | collective-permute-start | bytes 3080 | tf_op jit(solution)/shard_map/ppermute | solution.py:24
  4.8 9.9 %collective-permute-start.2 = (f32[2,128]{1,0:T(2,128)S(1)}, f32[2,128]{1,0:T(2,128)S(1)}, u32[]{:S(2)}, u32[]{:S(2)}) collective-permute-start(f32[2,128]{1,0:T(2,128)S(1)} %pad_maximum_fusion.5), channel_id=1, source_target_pairs={{1,0},{2,1},{3,2},{5,4},{6,5},{7,6},{9,8},{10,9},{11,10},{13,12},{... | collective-permute-start | bytes 3080 | tf_op jit(solution)/shard_map/ppermute | solution.py:24
  6.4 27.5 %copy-start.1 = (f32[128,128]{1,0:T(8,128)S(1)}, f32[128,128]{1,0:T(8,128)}, u32[]{:S(2)}) copy-start(f32[128,128]{1,0:T(8,128)} %param.10) | copy-start | bytes 196612
  6.4 27.5 %copy-start.2 = (s32[128,128]{1,0:T(8,128)S(1)}, s32[128,128]{1,0:T(8,128)}, u32[]{:S(2)}) copy-start(s32[128,128]{1,0:T(8,128)} %param.9) | copy-start | bytes 196612
  13.5 21.7 %copy-start.5 = (s32[128,128]{1,0:T(8,128)S(1)}, s32[128,128]{1,0:T(8,128)}, u32[]{:S(2)}) copy-start(s32[128,128]{1,0:T(8,128)} %param.13) | copy-start | bytes 196612
  20.2 14.0 %collective-permute-start = (f32[3,128]{1,0:T(4,128)S(1)}, f32[3,128]{1,0:T(4,128)S(1)}, u32[]{:S(2)}, u32[]{:S(2)}) collective-permute-start(f32[3,128]{1,0:T(4,128)S(1)} %pad_maximum_fusion.3), channel_id=1, source_target_pairs={{0,1},{1,2},{2,3},{4,5},{5,6},{6,7},{8,9},{9,10},{10,11},{12,13},{... | collective-permute-start | bytes 4616 | tf_op jit(solution)/shard_map/ppermute | solution.py:24
  28.3 6.8 %collective-permute-start.1 = (f32[3,128]{1,0:T(4,128)S(1)}, f32[3,128]{1,0:T(4,128)S(1)}, u32[]{:S(2)}, u32[]{:S(2)}) collective-permute-start(f32[3,128]{1,0:T(4,128)S(1)} %pad_maximum_fusion.4), channel_id=1, source_target_pairs={{0,4},{4,8},{8,12},{12,16},{16,20},{20,24},{24,28},{1,5},{5,9},{9,... | collective-permute-start | bytes 4616 | tf_op jit(solution)/shard_map/ppermute | solution.py:24
  40.3 2.2 %copy-start = (f32[5,128,128]{2,1,0:T(8,128)}, f32[5,128,128]{2,1,0:T(8,128)S(1)}, u32[]{:S(2)}) copy-start(f32[5,128,128]{2,1,0:T(8,128)S(1)} %bitcast_dynamic-update-slice_fusion.coef_ref) | copy-start | bytes 983044

commit v2 on v1

--- a/solution.py
+++ b/solution.py
@@ -18,37 +18,28 @@
     return jax.ShapeDtypeStruct(dims, F32)
 
 
-def shifted(value, axis, steps):
-    count = lax.axis_size(axis)
-    initial, last = (max(0, -steps), min(count, count - steps))
-    return lax.ppermute(value, axis, [(i, i + steps) for i in range(initial, last)])
-
-
-def lookup(entries, classes):
-    out = jnp.zeros(classes.shape, F32)
-    for k in range(entries.shape[0]):
-        out = jnp.where(classes == k, entries[k], out)
-    return out
-
-
 def sweep(size, out_ref):
-    lanes = lax.broadcasted_iota(jnp.int32, (size, size), 1)
-    rows = lax.broadcasted_iota(jnp.int32, (size, 1), 0)
-    row_lanes = lax.broadcasted_iota(jnp.int32, (1, size), 1)
-
-    def step(k, carry):
-        matrix = out_ref[...]
-        row = out_ref[pl.ds(k, 1), :]
-        pivot = jnp.sum(jnp.where(row_lanes == k, row, 0.0), axis=1, keepdims=True)
-        col = jnp.sum(jnp.where(lanes == k, matrix, 0.0), axis=1, keepdims=True)
-        recip = 1.0 / pivot
-        scaled = jnp.where(row_lanes == k, recip, row * recip)
-        kept = jnp.where(lanes == k, 0.0, matrix)
-        out_ref[...] = kept - jnp.where(rows == k, 0.0, col) * scaled
-        out_ref[pl.ds(k, 1), :] = scaled
-        return carry
-
-    lax.fori_loop(0, size, step, 0)
+    segment = 2 * REG
+    for start in range(0, size, segment):
+        reach = min(size, start + segment + 2 * REG)
+        width = size
+        lanes = lax.broadcasted_iota(jnp.int32, (reach, width), 1)
+        rows = lax.broadcasted_iota(jnp.int32, (reach, 1), 0)
+        row_lanes = lax.broadcasted_iota(jnp.int32, (1, width), 1)
+
+        def step(k, carry, reach=reach, width=width, lanes=lanes, rows=rows, row_lanes=row_lanes):
+            matrix = out_ref[:reach, :]
+            row = out_ref[pl.ds(k, 1), :]
+            pivot = jnp.sum(jnp.where(row_lanes == k, row, 0.0), axis=1, keepdims=True)
+            here = lanes == k
+            col = jnp.sum(jnp.where(here, matrix, 0.0), axis=1, keepdims=True)
+            recip = 1.0 / pivot
+            scaled = jnp.where(row_lanes == k, recip, row * recip)
+            out_ref[:reach, :] = jnp.where(here, 0.0, matrix) - jnp.where(rows == k, 0.0, col) * scaled
+            out_ref[pl.ds(k, 1), :] = scaled
+            return carry
+
+        lax.fori_loop(start, min(size, start + segment), step, 0)
 
 
 BLOCK = 32
@@ -143,8 +134,7 @@
     )(value)
 
 
-def exchange_kernel(rows, cols, *refs):
-    sources, landed, (send_sem, recv_sem) = refs[:4], refs[4:8], refs[8:]
+def exchange_kernel(rows, cols, x_ref, out_ref, send_sem, recv_sem):
     r, c = lax.axis_index("row"), lax.axis_index("col")
     targets = (
         (lax.rem(r + 1, rows), c),
@@ -158,8 +148,8 @@
     pl.semaphore_wait(barrier, 4)
     copies = [
         pltpu.make_async_remote_copy(
-            src_ref=sources[k],
-            dst_ref=landed[k],
+            src_ref=x_ref.at[k],
+            dst_ref=out_ref.at[k],
             send_sem=send_sem.at[k],
             recv_sem=recv_sem.at[k],
             device_id=targets[k],
@@ -173,15 +163,15 @@
         copy.wait()
 
 
-def exchange(values, ident):
+def exchange(value, ident):
     return pl.pallas_call(
         functools.partial(exchange_kernel, lax.axis_size("row"), lax.axis_size("col")),
-        out_shape=tuple(shape(*v.shape) for v in values),
-        in_specs=[VM] * 4,
-        out_specs=(VM,) * 4,
+        out_shape=shape(*value.shape),
+        in_specs=[VM],
+        out_specs=VM,
         scratch_shapes=[pltpu.SemaphoreType.DMA((4,)), pltpu.SemaphoreType.DMA((4,))],
         compiler_params=pltpu.CompilerParams(collective_id=ident, has_side_effects=True),
-    )(*values)
+    )(value)
 
 
 def matrix_kernel(plan, gathered_ref, place_ref, out_ref):
@@ -293,6 +283,88 @@
     return [cx_ref[b, (part + a) * n : (part + a + 1) * n, :] for a in (0, 1) for b in (0, 1)]
 
 
+def looked_up(table_ref, classes):
+    out = jnp.zeros(classes.shape, F32)
+    for k in range(table_ref.shape[0]):
+        out = jnp.where(classes == k, table_ref[k], out)
+    return out
+
+
+def links_kernel(plan, h_ref, v_ref, label_ref, bump_ref, table_ref, link_ref, edge_ref):
+    rows, cols = h_ref.shape
+    last_row = lax.axis_index("row") == lax.axis_size("row") - 1
+    last_col = lax.axis_index("col") == lax.axis_size("col") - 1
+    i = lax.broadcasted_iota(jnp.int32, (rows, cols), 0)
+    j = lax.broadcasted_iota(jnp.int32, (rows, cols), 1)
+    row_end = jnp.where(last_row, rows - 1, rows)
+    col_end = jnp.where(last_col, cols - 1, cols)
+    right = jnp.where(j == col_end, 0.0, looked_up(table_ref, h_ref[...]))
+    down = jnp.where(i == row_end, 0.0, looked_up(table_ref, v_ref[...]))
+    link_ref[0] = right
+    link_ref[1] = down
+    edge_ref[...] = jnp.zeros_like(edge_ref)
+    named = label_ref[...].astype(F32)
+    bump = bump_ref[...]
+    for k, value in enumerate((named, bump, down)):
+        edge_ref[0, k : k + 1, :] = value[rows - 1 :]
+        edge_ref[1, k : k + 1, :] = value[:1]
+    for k, value in enumerate((named, bump, right)):
+        turned = value.T
+        edge_ref[2, k : k + 1, :] = turned[cols - 1 :]
+        edge_ref[3, k : k + 1, :] = turned[:1]
+
+
+def masks_kernel(plan, width, link_ref, edge_ref, label_ref, bump_ref, pad_ref, table_ref, mask_ref, image_ref, coef_ref):
+    rows, cols = label_ref.shape
+    i = lax.broadcasted_iota(jnp.int32, (rows, cols), 0)
+    j = lax.broadcasted_iota(jnp.int32, (rows, cols), 1)
+
+    def at_left(value, k):
+        return jnp.where(j == 0, jnp.broadcast_to(edge_ref[2, k : k + 1, :], (cols, rows)).T, pltpu.roll(value, 1, 1))
+
+    def at_right(value, k):
+        return jnp.where(j == cols - 1, jnp.broadcast_to(edge_ref[3, k : k + 1, :], (cols, rows)).T, pltpu.roll(value, cols - 1, 1))
+
+    def at_top(value, k):
+        return jnp.where(i == 0, edge_ref[0, k : k + 1, :], pltpu.roll(value, 1, 0))
+
+    def at_low(value, k):
+        return jnp.where(i == rows - 1, edge_ref[1, k : k + 1, :], pltpu.roll(value, rows - 1, 0))
+
+    right, down = link_ref[0], link_ref[1]
+    left, upper = at_left(right, 2), at_top(down, 2)
+    diagonal = looked_up(table_ref, pad_ref[...]) + right + left + down + upper
+    for k, value in enumerate((diagonal, right, left, down, upper)):
+        coef_ref[k] = value
+    tile_row = (lax.axis_index("row") * (rows // plan.height) - 1).astype(F32)
+    tile_col = (lax.axis_index("col") * (cols // width) - 1).astype(F32)
+    base_row = jnp.zeros((rows, cols), F32) + tile_row
+    base_col = jnp.zeros((rows, cols), F32) + tile_col
+    for p in range(1, plan.parts):
+        base_row = base_row + jnp.where(i >= p * plan.height - plan.height // 2, 1.0, 0.0)
+    for p in range(1, cols // width + 1):
+        base_col = base_col + jnp.where(j >= p * width - width // 2, 1.0, 0.0)
+    named, bump = label_ref[...].astype(F32), bump_ref[...]
+    total = None
+    for label, weight in (
+        (named, diagonal * bump),
+        (at_right(named, 0), -right * at_right(bump, 1)),
+        (at_left(named, 0), -left * at_left(bump, 1)),
+        (at_low(named, 0), -down * at_low(bump, 1)),
+        (at_top(named, 0), -upper * at_top(bump, 1)),
+    ):
+        high = jnp.floor(label * (1.0 / REG))
+        a, b = high - base_row, label - REG * high - base_col
+        hits = [(a == m) & (b == n) for m in (0.0, 1.0) for n in (0.0, 1.0)]
+        if total is None:
+            for k in range(4):
+                mask_ref[k] = jnp.where(hits[k], bump, 0.0)
+        terms = [jnp.where(hit, weight, 0.0) for hit in hits]
+        total = terms if total is None else [t + u for t, u in zip(total, terms)]
+    for k in range(4):
+        image_ref[k] = total[k]
+
+
 def sums_kernel(plan, b_ref, mask_ref, image_ref, hot_ref, out_ref, s_ref, pair_ref):
     n = plan.loads
     s_ref[...] = jnp.zeros_like(s_ref)
@@ -349,17 +421,19 @@
 
         carry = over_rows(first, last, step, carry)
     rho_ref[0] = carry[0]
-    edge_ref[0] = carry[1]
-    edge_ref[1] = carry[2]
-
-
-def image_kernel(plan, z_ref, above_ref, below_ref, left_ref, right_ref, coef_ref, mask_ref, hot_ref, dots_ref, f_ref, out_ref, s_ref):
+    edge_ref[0] = z_ref[(plan.rows - 1) * n :, :]
+    edge_ref[1] = z_ref[:n, :]
+    edge_ref[2] = carry[2]
+    edge_ref[3] = carry[1]
+
+
+def image_kernel(plan, z_ref, edge_ref, coef_ref, mask_ref, hot_ref, dots_ref, f_ref, out_ref, s_ref):
     n = plan.loads
     cols = z_ref.shape[-1]
     zero = jnp.zeros((n, cols), F32)
     lane = lax.broadcasted_iota(jnp.int32, (n, cols), 1)
     s_ref[...] = jnp.zeros_like(s_ref)
-    left_pack, right_pack = left_ref[...], right_ref[...]
+    left_pack, right_pack = edge_ref[2], edge_ref[3]
 
     def image(i, z, up, down):
         before = jnp.where(lane == 0, pltpu.roll(left_pack, lax.rem(cols - i, cols), 1), pltpu.roll(z, 1, 1))
@@ -389,13 +463,16 @@
         carry = (zf,) + (zero,) * 4
         low, high = first, last
         if first == 0:
-            carry = finish(0, load(0), above_ref[...], load(1), carry)
+            carry = finish(0, load(0), edge_ref[0], load(1), carry)
             low = 1
         if last == plan.rows:
             high = last - 1
-        carry = over_rows(low, high, step, carry, 1 if (high - low) % 4 else 4)
+        while (high - low) % 4:
+            carry = step(low, carry)
+            low += 1
+        carry = over_rows(low, high, step, carry)
         if last == plan.rows:
-            carry = finish(last - 1, load(last - 1), load(last - 2), below_ref[...], carry)
+            carry = finish(last - 1, load(last - 1), load(last - 2), edge_ref[1], carry)
         zf, *acc = carry
         add_sums(plan, s_ref, part, acc)
     out_ref[...] = pack(hot_ref, s_ref, [dots_ref[k] for k in range(dots_ref.shape[0])] + [zf])
@@ -423,8 +500,10 @@
         carry = over_rows(first, last, step, carry)
     dots_ref[0] = carry[0]
     dots_ref[1] = carry[1]
-    edge_ref[0] = carry[2]
-    edge_ref[1] = carry[3]
+    edge_ref[0] = z1_ref[(plan.rows - 1) * n :, :]
+    edge_ref[1] = z1_ref[:n, :]
+    edge_ref[2] = carry[3]
+    edge_ref[3] = carry[2]
 
 
 def last_kernel(plan, z_ref, z1_ref, r1_ref, f1_ref, q_ref, mask_ref, image_ref, cs_ref, cx_ref, scal_ref, s_out, r_out):
@@ -455,52 +534,22 @@
     plan = Plan(rows, loads, height)
     levels = plan.levels
     ri, ci = lax.axis_index("row"), lax.axis_index("col")
-    row_ids = ri * rows + lax.broadcasted_iota(jnp.int32, (rows, cols), 0)
-    col_ids = ci * cols + lax.broadcasted_iota(jnp.int32, (rows, cols), 1)
-    right_link = jnp.where(col_ids == grid_cols - 1, 0.0, lookup(edge_table, horizontal_class))
-    down_link = jnp.where(row_ids == grid_rows - 1, 0.0, lookup(edge_table, vertical_class))
-    named = labels.astype(F32)
-    right_end = jnp.stack([named[:, -1], bump_height[:, -1], right_link[:, -1]])
-    left_end = jnp.stack([named[:, 0], bump_height[:, 0]])
-    low_end = jnp.stack([named[-1], bump_height[-1], down_link[-1]])
-    top_end = jnp.stack([named[0], bump_height[0]])
-    before = shifted(right_end, "col", 1)
-    after = shifted(left_end, "col", -1)
-    above = shifted(low_end, "row", 1)
-    below = shifted(top_end, "row", -1)
-
-    def at_left(value, k):
-        return jnp.concatenate([before[k][:, None], value[:, :-1]], axis=1)
-
-    def at_right(value, k):
-        return jnp.concatenate([value[:, 1:], after[k][:, None]], axis=1)
-
-    def at_top(value, k):
-        return jnp.concatenate([above[k][None], value[:-1]], axis=0)
-
-    def at_low(value, k):
-        return jnp.concatenate([value[1:], below[k][None]], axis=0)
-
-    left_link = at_left(right_link, 2)
-    upper_link = at_top(down_link, 2)
-    diagonal = lookup(pad_table, pad_class) + right_link + left_link + down_link + upper_link
-    base_row = (row_ids + height // 2) // height - 1
-    base_col = (col_ids + width // 2) // width - 1
-
-    def masks(name, weight):
-        name = name.astype(jnp.int32)
-        a, b = name // REG - base_row, name % REG - base_col
-        return jnp.stack([jnp.where((a == i) & (b == j), weight, 0.0) for i in (0, 1) for j in (0, 1)])
-
-    mask = masks(named, bump_height)
-    image = (
-        masks(named, diagonal * bump_height)
-        - masks(at_right(named, 0), right_link * at_right(bump_height, 1))
-        - masks(at_left(named, 0), left_link * at_left(bump_height, 1))
-        - masks(at_low(named, 0), down_link * at_low(bump_height, 1))
-        - masks(at_top(named, 0), upper_link * at_top(bump_height, 1))
-    )
-    coef = jnp.stack([diagonal, right_link, left_link, down_link, upper_link])
+    smem = pl.BlockSpec(memory_space=pltpu.SMEM)
+    links, ends = pl.pallas_call(
+        functools.partial(links_kernel, plan),
+        out_shape=(shape(2, rows, cols), shape(4, 8, cols)),
+        in_specs=[VM] * 4 + [smem],
+        out_specs=(VM, VM),
+        compiler_params=PARAMS,
+    )(horizontal_class, vertical_class, labels, bump_height, edge_table)
+    ends = exchange(ends, 5)
+    mask, image, coef = pl.pallas_call(
+        functools.partial(masks_kernel, plan, width),
+        out_shape=(shape(4, rows, cols), shape(4, rows, cols), shape(5, rows, cols)),
+        in_specs=[VM] * 5 + [smem],
+        out_specs=(VM,) * 3,
+        compiler_params=PARAMS,
+    )(links, ends, labels, bump_height, pad_class, pad_table)
 
     span = cols // width + 2
     lane_base = (lax.iota(jnp.int32, cols) + width // 2) // width
@@ -536,8 +585,8 @@
     coarse_shape = shape(regions, 4 * BLOCK)
 
     def image_of(z, edges, dots, ident):
-        landed = exchange((z[-loads:], z[:loads], edges[1], edges[0]), ident)
-        f, sums = call(image_kernel, (field, message), z, *landed, coef, mask, hot, dots, scratch=sums_scratch)
+        landed = exchange(edges, ident)
+        f, sums = call(image_kernel, (field, message), z, landed, coef, mask, hot, dots, scratch=sums_scratch)
         return f, gather(sums, ident + 1).reshape(count * 8, 4 * BLOCK)
 
     flat = load_currents.reshape(loads * rows, cols)
@@ -546,7 +595,7 @@
     inverse = call(matrix_kernel, shape(regions, regions), first[:, 1].reshape(count * 8, 4 * BLOCK), place)
     cx, c0 = call(solve_first, (s_shape, coarse_shape), first[:, 0].reshape(count * 8, 4 * BLOCK), place, inverse, expand)
     r0, z0, rho_lanes, edges = call(
-        first_kernel, (field, field, shape(1, loads, cols), shape(2, loads, cols)), flat, image, coef, cx
+        first_kernel, (field, field, shape(1, loads, cols), shape(4, loads, cols)), flat, image, coef, cx
     )
     f0, sums = image_of(z0, edges, rho_lanes, 1)
     cx, c1, scal, alpha = call(
@@ -554,7 +603,7 @@
     )
     r1, z1, q0, dots, edges = call(
         second_kernel,
-        (field, field, field, shape(2, loads, cols), shape(2, loads, cols)),
+        (field, field, field, shape(2, loads, cols), shape(4, loads, cols)),
         r0, f0, image, coef, cx, alpha,
     )
     f1, sums = image_of(z1, edges, dots, 3)

time: 207 us -> 162 us (0.78)
  other arithmetic: 21.6 us -> 3.12 us
  local copies, waits for them, and re-layouts: 15.3 us -> 1.69 us
  starting transfers between devices: 11.1 us -> 0 us
    another operation x14 -> x0, other arithmetic: 11.3 us -> none  [the longest x9 11.2 us: masks(): jnp.stack([jnp.where((a == i) & (b == j), weight, 0.0) for i in (0, 1) fo...]
    ppermute x4 -> x0, starting transfers between devices: 11.1 us -> none  [shifted(): lax.ppermute(value, axis, [(i, i + steps) for i in range(initial, last)])]
    pallas_call x10, Pallas kernels: 104 us -> 92.7 us  [call(): pl.pallas_call(functools.partial(kernel, plan), out_shape=outs, in_specs=...]
    pallas_call x2 -> x3, Pallas kernels: 18.4 us -> 28.6 us  [exchange(): pl.pallas_call(functools.partial(exchange_kernel, lax.axis_size('row'), l...]
    slice x10 -> x0, local copies, waits for them, and re-layouts: 8.1 us -> none  [the longest x2 3.26 us: lookup(): out = jnp.where(classes == k, entries[k], out)]
    unnamed x2 -> x0, other arithmetic: 5.05 us -> none
    pallas_call x0 -> x2, Pallas kernels: none -> 3.95 us  [the longest x1 2.22 us: body(): pl.pallas_call(functools.partial(masks_kernel, plan, width), out_shape=(s...]
    pallas_call x3, Pallas kernels: 34.1 us -> 31 us  [gather(): pl.pallas_call(functools.partial(gather_kernel, rows, cols), out_shape=sh...]
  transfers between devices with their start and end apart: 4 -> 0, of which waited for: 1 -> 0; matrix products, arithmetic and copies ran while one was open for 10% -> 0% of each run, Pallas kernels for 0% -> 0%
where the time goes in v2:
time: 162 us
  Pallas kernels  156 us (96%)
  other arithmetic  3.12 us (2%)
  local copies, waits for them, and re-layouts  1.69 us (1%)
    pallas_call x10, Pallas kernels, call(): pl.pallas_call(functools.partial(kernel, plan), out_shape=outs, in_specs=...  92.7 us
    pallas_call x3, Pallas kernels, gather(): pl.pallas_call(functools.partial(gather_kernel, rows, cols), out_shape=sh...  31 us
    pallas_call x3, Pallas kernels, exchange(): pl.pallas_call(functools.partial(exchange_kernel, lax.axis_size('row'), l...  28.6 us

profile of v2, /device:TPU:0, one launch (start us, length us, event | category | flops | bytes accessed | tf_op | source)
XLA Modules:
  0.0 161.8 jit_solution(11233528058185332982)
XLA Ops:
  0.8 0.6 add_convert_fusion.hot_ref
  1.4 1.7 %shard_map.95 = (f32[2,128,128]{2,1,0:T(8,128)}, f32[4,8,128]{2,1,0:T(8,128)}) custom-call(s32[128,128]{1,0:T(8,128)} %h_ref.1, s32[128,128]{1,0:T(8,128)} %v_ref.1, s32[128,128]{1,0:T(8,128)} %label_ref.3, f32[128,128]{1,0:T(8,128)} %bump_ref.3, f32[8]{0:T(128)} %table_ref.2), custom_call_target="tpu_custom_call" | custom-call | tf_op jit(solution)/shard_map/pallas_call | solution.py:538
  3.1 10.0 %shard_map.96.edge_ref = f32[4,8,128]{2,1,0:T(8,128)} custom-call(f32[4,8,128]{2,1,0:T(8,128)} %get-tuple-element.32.x_ref), custom_call_target="tpu_custom_call" | custom-call | tf_op jit(solution)/shard_map/pallas_call | solution.py:167
  13.1 1.3 fusion.19.place_ref
  14.4 1.2 fusion.16.expand_ref
  15.5 2.2 %shard_map.97 = (f32[4,128,128]{2,1,0:T(8,128)}, f32[4,128,128]{2,1,0:T(8,128)}, f32[5,128,128]{2,1,0:T(8,128)}) custom-call(f32[2,128,128]{2,1,0:T(8,128)} %get-tuple-element.31.link_ref, f32[4,8,128]{2,1,0:T(8,128)} %shard_map.96.edge_ref, s32[128,128]{1,0:T(8,128)} %label_ref.3, f32[128,128]{1,0:T(8,128)} %bump_ref.3, s32[128,128]{1,0:T(8,128)} %pad_ref.1, ...), custom_call_target="tpu_custom_call" | custom-call | tf_op jit(solution)/shard_map/pallas_call | solution.py:546
  17.8 4.5 %shard_map.98.x_ref = f32[2,8,128]{2,1,0:T(8,128)} custom-call(f32[4096,128]{1,0:T(8,128)} %bitcast.9, f32[4,128,128]{2,1,0:T(8,128)} %get-tuple-element.35.mask_ref, f32[4,128,128]{2,1,0:T(8,128)} %get-tuple-element.33.image_ref, f32[2,8,128]{2,1,0:T(8,128)} %add_convert_fusion.hot_ref), custom_call_target="tpu_custom_call" | custom-call | tf_op jit(solution)/shard_map/pallas_call | solution.py:572
  22.3 11.7 %shard_map.99 = f32[32,2,8,128]{3,2,1,0:T(8,128)} custom-call(f32[2,8,128]{2,1,0:T(8,128)} %shard_map.98.x_ref), custom_call_target="tpu_custom_call" | custom-call | tf_op jit(solution)/shard_map/pallas_call | solution.py:127
  34.0 1.7 %slice_bitcast_fusion = (f32[256,128]{1,0:T(8,128)}, f32[256,128]{1,0:T(8,128)}) fusion(f32[32,2,8,128]{3,2,1,0:T(8,128)} %shard_map.99), kind=kLoop, calls=%fused_computation.54 | loop fusion | bytes 524288 | tf_op jit(solution)/shard_map/reshape;squeeze | solution.py:595
  35.7 33.0 %shard_map.100.inverse_ref = f32[256,256]{1,0:T(8,128)} custom-call(f32[256,128]{1,0:T(8,128)} %get-tuple-element.60.gathered_ref, bf16[256,1024]{1,0:T(8,128)(2,1)} %fusion.19.place_ref), custom_call_target="tpu_custom_call" | custom-call | tf_op jit(solution)/shard_map/pallas_call | solution.py:572
  68.7 3.8 %shard_map.101 = (f32[2,128,128]{2,1,0:T(8,128)}, f32[256,128]{1,0:T(8,128)}) custom-call(f32[256,128]{1,0:T(8,128)} %get-tuple-element.61.gathered_ref, bf16[256,1024]{1,0:T(8,128)(2,1)} %fusion.19.place_ref, f32[256,256]{1,0:T(8,128)} %shard_map.100.inverse_ref, bf16[256,1024]{1,0:T(8,128)(2,1)} %fusion.16.expand_ref), custom_call_target="tpu_custom_call" | custom-call | tf_op jit(solution)/shard_map/pallas_call | solution.py:572
  72.5 8.0 %shard_map.102 = (f32[4096,128]{1,0:T(8,128)}, f32[4096,128]{1,0:T(8,128)}, f32[1,32,128]{2,1,0:T(8,128)}, f32[4,32,128]{2,1,0:T(8,128)}) custom-call(f32[4096,128]{1,0:T(8,128)} %bitcast.10, f32[4,128,128]{2,1,0:T(8,128)} %get-tuple-element.33.image_ref, f32[5,128,128]{2,1,0:T(8,128)} %get-tuple-element.34.coef_ref, f32[2,128,128]{2,1,0:T(8,128)} %get-tuple-element.36.cx_ref), custom_call_target="tpu_custom_call" | custom-call | tf_op jit(solution)/shard_map/pallas_call | solution.py:572
  80.4 9.8 %shard_map.103.edge_ref = f32[4,32,128]{2,1,0:T(8,128)} custom-call(f32[4,32,128]{2,1,0:T(8,128)} %get-tuple-element.39.x_ref), custom_call_target="tpu_custom_call" | custom-call | tf_op jit(solution)/shard_map/pallas_call | solution.py:167
  90.2 7.9 %shard_map.104 = (f32[4096,128]{1,0:T(8,128)}, f32[8,128]{1,0:T(8,128)}) custom-call(f32[4096,128]{1,0:T(8,128)} %get-tuple-element.37.z_ref, f32[4,32,128]{2,1,0:T(8,128)} %shard_map.103.edge_ref, f32[5,128,128]{2,1,0:T(8,128)} %get-tuple-element.34.coef_ref, f32[4,128,128]{2,1,0:T(8,128)} %get-tuple-element.35.mask_ref, ...), custom_call_target="tpu_custom_call" | custom-call | tf_op jit(solution)/shard_map/pallas_call | solution.py:572
  98.1 9.7 %shard_map.105 = f32[32,8,128]{2,1,0:T(8,128)} custom-call(f32[8,128]{1,0:T(8,128)} %get-tuple-element.42.x_ref), custom_call_target="tpu_custom_call" | custom-call | tf_op jit(solution)/shard_map/pallas_call | solution.py:127
  107.8 3.8 %shard_map.106 = (f32[2,128,128]{2,1,0:T(8,128)}, f32[256,128]{1,0:T(8,128)}, f32[8,128]{1,0:T(8,128)}, f32[32,128]{1,0:T(8,128)}) custom-call(f32[256,128]{1,0:T(8,128)} %bitcast.12, bf16[256,1024]{1,0:T(8,128)(2,1)} %fusion.19.place_ref, f32[256,256]{1,0:T(8,128)} %shard_map.100.inverse_ref, bf16[256,1024]{1,0:T(8,128)(2,1)} %fusion.16.expand_ref), custom_call_target="tpu_custom_call" | custom-call | tf_op jit(solution)/shard_map/pallas_call | solution.py:572
  111.5 8.6 %shard_map.107 = (f32[4096,128]{1,0:T(8,128)}, f32[4096,128]{1,0:T(8,128)}, f32[4096,128]{1,0:T(8,128)}, f32[2,32,128]{2,1,0:T(8,128)}, f32[4,32,128]{2,1,0:T(8,128)}) custom-call(f32[4096,128]{1,0:T(8,128)} %get-tuple-element.38.r_ref, f32[4096,128]{1,0:T(8,128)} %get-tuple-element.41.f_ref, f32[4,128,128]{2,1,0:T(8,128)} %get-tuple-element.33.image_ref, ...), custom_call_target="tpu_custom_call" | custom-call | tf_op jit(solution)/shard_map/pallas_call | solution.py:572
  120.1 8.8 %shard_map.108.edge_ref = f32[4,32,128]{2,1,0:T(8,128)} custom-call(f32[4,32,128]{2,1,0:T(8,128)} %get-tuple-element.47.x_ref), custom_call_target="tpu_custom_call" | custom-call | tf_op jit(solution)/shard_map/pallas_call | solution.py:167
  129.0 8.0 %shard_map.109 = (f32[4096,128]{1,0:T(8,128)}, f32[8,128]{1,0:T(8,128)}) custom-call(f32[4096,128]{1,0:T(8,128)} %get-tuple-element.45.z_ref.z1_ref, f32[4,32,128]{2,1,0:T(8,128)} %shard_map.108.edge_ref, f32[5,128,128]{2,1,0:T(8,128)} %get-tuple-element.34.coef_ref, f32[4,128,128]{2,1,0:T(8,128)} %get-tuple-element.35.mask_ref, ...), custom_call_target="tpu_custom_call" | custom-call | tf_op jit(solution)/shard_map/pallas_call | solution.py:572
  136.9 9.7 %shard_map.110 = f32[32,8,128]{2,1,0:T(8,128)} custom-call(f32[8,128]{1,0:T(8,128)} %get-tuple-element.51.x_ref), custom_call_target="tpu_custom_call" | custom-call | tf_op jit(solution)/shard_map/pallas_call | solution.py:127
  146.6 4.0 %shard_map.111 = (f32[2,128,128]{2,1,0:T(8,128)}, f32[2,128,128]{2,1,0:T(8,128)}, f32[3,32,128]{2,1,0:T(8,128)}) custom-call(f32[256,128]{1,0:T(8,128)} %bitcast.11, bf16[256,1024]{1,0:T(8,128)(2,1)} %fusion.19.place_ref, f32[256,256]{1,0:T(8,128)} %shard_map.100.inverse_ref, bf16[256,1024]{1,0:T(8,128)(2,1)} %fusion.16.expand_ref, ...), custom_call_target="tpu_custom_call" | custom-call | tf_op jit(solution)/shard_map/pallas_call | solution.py:572
  150.7 11.1 %shard_map.112 = (f32[4096,128]{1,0:T(8,128)}, f32[4096,128]{1,0:T(8,128)}) custom-call(f32[4096,128]{1,0:T(8,128)} %get-tuple-element.37.z_ref, f32[4096,128]{1,0:T(8,128)} %get-tuple-element.45.z_ref.z1_ref, f32[4096,128]{1,0:T(8,128)} %get-tuple-element.46.r1_ref, f32[4096,128]{1,0:T(8,128)} %get-tuple-element.49.f1_ref, ...), custom_call_target="tpu_custom_call" | custom-call | tf_op jit(solution)/shard_map/pallas_call | solution.py:572
  (14 shorter events, 0.1 us)
